TPU v7x, 256 devices: a whole 4x4x8 slice. The times are simulated.
256 devices in a mesh: tower: 8 (over z), dev: 32 (over x, y, core).
Axes of the slice: x: 4, y: 4, z: 8, core: 2. Of those that a mesh axis runs over, the one named last changes fastest.
Arguments:
- grad_out: bfloat16 [8192, 8, 256], P(('tower', 'dev')), may hold values from -6 to 6
- pooled: bfloat16 [8, 32, 256, 1024], P('tower', 'dev'), may hold values from -6 to 6
- compress_w: bfloat16 [8, 1024, 256], P('tower'), may hold values from -0.1875 to 0.1875
- owner_ids: int32 [8, 32, 8192, 1], P('tower', 'dev'), may hold values from 0 to 31; in each aligned block of 8192 rows (0 to 8191, 8192 to 16383, ..., all dimensions but the last counted through in order) at most 512 rows name the same one
- slot_ids: int32 [8, 32, 8192], P('tower', 'dev'), may hold values from 0 to 1023
- touched: int32 [8, 32, 1024], P('tower', 'dev'), may hold values from 0 to 4095, as said below
- table: float32 [8, 131072, 128], P('tower', 'dev'), may hold values from -6 to 6
- accum: float32 [8, 131072], P('tower', 'dev'), may hold values from 0.05 to 2
Outputs:
- grad_compress: float32 [8, 1024, 256], P('tower', 'dev')
- new_table: float32 [8, 131072, 128], P('tower', 'dev')
- new_accum: float32 [8, 131072], P('tower', 'dev')
Inputs may be any that keep to these rules, and one draw needn't show every extreme that they name: `owner_ids`: the 8192 occurrences of one device name one owner at most 512 times. `touched`: the 1024 entries of one owner are distinct rows.
All inputs are finite; a program needn't handle non-finite values.
Results may differ from a plain program's by a relative error of at most 0.0029.
Values may be sent and summed in bfloat16 or wider, within the bound.
A program may use at most 64 MiB of HBM per device.

v0:
```python
import math

import jax
import jax.numpy as jnp
from jax import lax
from jax.sharding import PartitionSpec as P

E = 128
HOT = 4


learn_rate = 0.1
epsilon = 1e-06
highest = lax.Precision.HIGHEST


def count_before(matches):
    row_total, length = matches.shape
    width = math.gcd(length, 128)
    blocks = length // width
    marks = matches.astype(jnp.bfloat16).reshape(row_total, blocks, width)
    lower = lax.broadcasted_iota(jnp.int32, (width, width), 0)
    upper = lax.broadcasted_iota(jnp.int32, (width, width), 1)
    inclusive = (lower <= upper).astype(jnp.bfloat16)
    within = jnp.einsum("rbi,ij->rbj", marks, inclusive, preferred_element_type=jnp.float32)
    totals = within[:, :, width - 1]
    block_a = lax.broadcasted_iota(jnp.int32, (blocks, blocks), 0)
    block_b = lax.broadcasted_iota(jnp.int32, (blocks, blocks), 1)
    strict = (block_a < block_b).astype(jnp.float32)
    offsets = jnp.dot(totals, strict, precision=highest, preferred_element_type=jnp.float32)
    ranks = within + offsets[:, :, None]
    return ranks.reshape(row_total, length).astype(jnp.int32) - 1


def accumulate(values, slot_flat, touch_count):
    total_rows = values.shape[0]
    block_size = math.gcd(total_rows, 4096)
    block_count = total_rows // block_size
    value_blocks = values.reshape(block_count, block_size, values.shape[1])
    slot_blocks = slot_flat.reshape(block_count, block_size)
    targets = lax.broadcasted_iota(jnp.int32, (touch_count, block_size), 0)

    def add_block(totals, block_pair):
        onehot = (block_pair[1][None, :] == targets).astype(jnp.bfloat16)
        return (totals + jnp.dot(onehot, block_pair[0], preferred_element_type=jnp.float32), None)

    start_sum = jnp.zeros((touch_count, values.shape[1]), jnp.float32)
    result, unused = lax.scan(add_block, start_sum, (value_blocks, slot_blocks))
    return result


def shards(grad_out, pooled, compress_w, owner_ids, slot_ids, touched, table, accum):
    owners = lax.axis_size("dev")
    moved = lax.all_to_all(grad_out, "tower", split_axis=1, concat_axis=0, tiled=True)
    grad_tower = moved[:, 0, :]
    pooled_rows = pooled[0, 0]
    weight = compress_w[0]
    preact = jnp.dot(pooled_rows, weight, preferred_element_type=jnp.float32)
    sigma = jax.nn.sigmoid(preact)
    grad_pre = (grad_tower.astype(jnp.float32) * sigma * (1.0 + preact * (1.0 - sigma))).astype(
        jnp.bfloat16
    )
    occurrences = owner_ids.shape[2]
    capacity = 2 * occurrences // owners
    touch_count = touched.shape[2]
    slot_total = owners * capacity
    bag_rows = (
        lax.dot_general(
            grad_pre, weight, (((1,), (1,)), ((), ())), preferred_element_type=jnp.float32
        )
        .astype(jnp.bfloat16)
        .reshape(-1, E)
    )
    occ_values = jnp.repeat(bag_rows, HOT, axis=0)
    targets_own = owner_ids[0, 0, :, 0]
    slots_own = slot_ids[0, 0]
    owner_iota = lax.broadcasted_iota(jnp.int32, (owners, occurrences), 0)
    matches = targets_own[None, :] == owner_iota
    ranks = count_before(matches)
    own_rank = jnp.sum(jnp.where(matches, ranks, 0), axis=0)
    dest = targets_own * capacity + own_rank
    send_values = jnp.zeros((slot_total, E), jnp.bfloat16).at[dest].set(occ_values, mode="drop")
    row_slots = jnp.full((slot_total,), -1, jnp.int32).at[dest].set(slots_own, mode="drop")
    send_values = send_values.reshape(owners, capacity, E)
    row_slots = row_slots.reshape(owners, capacity)
    recv_values, recv_slots = (
        lax.all_to_all(send_values, "dev", split_axis=0, concat_axis=0, tiled=True),
        lax.all_to_all(row_slots, "dev", split_axis=0, concat_axis=0, tiled=True),
    )
    row_grad = accumulate(recv_values.reshape(-1, E), recv_slots.reshape(-1), touch_count)
    sq_mean = jnp.mean(row_grad * row_grad, axis=1)
    local_rows = touched[0, 0]
    accum_local = accum[0]
    table_local = table[0]
    accum_touched = accum_local[local_rows] + sq_mean
    updated = (
        table_local[local_rows] - learn_rate * row_grad / jnp.sqrt(accum_touched + epsilon)[:, None]
    )
    new_table = table_local.at[local_rows].set(updated)
    new_accum = accum_local.at[local_rows].set(accum_touched)
    grad_weight = lax.psum_scatter(
        lax.dot_general(
            pooled_rows, grad_pre, (((0,), (0,)), ((), ())), preferred_element_type=jnp.float32
        ),
        "dev",
        scatter_dimension=0,
        tiled=True,
    )
    return (grad_weight[None], new_table[None], new_accum[None])


def solution(mesh):
    return jax.shard_map(
        shards,
        mesh=mesh,
        in_specs=(
            P(("tower", "dev"), None, None),
            P("tower", "dev", None, None),
            P("tower", None, None),
            P("tower", "dev", None, None),
            P("tower", "dev", None),
            P("tower", "dev", None),
            P("tower", "dev", None),
            P("tower", "dev"),
        ),
        out_specs=(P("tower", "dev", None), P("tower", "dev", None), P("tower", "dev")),
        check_vma=False,
    )
```

profile of v0, /device:TPU:1, one launch (start us, length us, event | category | flops | bytes accessed | tf_op | source)
XLA Modules:
  0.0 222.0 jit_solution(4723609337550919614)
XLA Ops:
  7.2 0.0 copy-start
  7.2 0.8 copy.30
  8.0 0.9 copy-done.7
  8.9 0.7 copy.15
  9.5 9.1 %all-to-all-start = ((bf16[32,8,256]{2,0,1:T(8,128)(2,1)}), bf16[32,8,256]{2,0,1:T(8,128)(2,1)S(1)}, u32[]{:S(2)}, u32[]{:S(2)}) async-start(bf16[32,8,256]{2,0,1:T(8,128)(2,1)} %copy.15), calls=%async_computation | async-start | bytes 262144 | tf_op jit(solution)/shard_map/all_to_all | solution.py:54
  18.7 0.0 copy-done.6
  18.7 0.3 fusion.10
  19.0 0.6 slice_reduce_fusion
  19.6 0.1 fusion.33
  19.8 0.4 select_reduce_fusion
  20.1 0.1 compare_select_fusion
  20.2 31.2 %scatter_custom_fusion = s32[16384]{0:T(1024)} fusion(s32[8192]{0:T(1024)S(1)} %bitcast.77, s32[8192]{0:T(1024)} %bitcast.79, s32[]{:T(128)} %constant.8.clone.1), kind=kCustom, calls=%fused_computation.45 | custom fusion | bytes 66048 | tf_op jit(solution)/shard_map/scatter | solution.py:83
  51.4 0.0 all-to-all-done
  51.4 8.0 %all-to-all-start.1 = ((s32[32,1,512]{2,1,0:T(1,128)}), s32[32,1,512]{2,1,0:T(1,128)S(1)}, u32[]{:S(2)}, u32[]{:S(2)}) async-start(s32[32,1,512]{2,1,0:T(1,128)} %bitcast.16), calls=%async_computation.1 | async-start | bytes 131072 | tf_op jit(solution)/shard_map/all_to_all | solution.py:88
  59.5 0.0 copy-done
  59.5 0.0 copy-done.4
  59.5 0.3 fusion.22
  59.9 0.3 convolution_convert_fusion
  60.2 0.2 reshape.110
  60.5 0.6 broadcast_in_dim.39
  61.1 23.6 %scatter_custom_fusion.1 = bf16[16384,128]{1,0:T(8,128)(2,1)} fusion(s32[8192]{0:T(1024)S(1)} %bitcast.78, bf16[8192,128]{1,0:T(8,128)(2,1)S(1)} %bitcast.68, bf16[]{:T(256)} %constant.21.clone.1), kind=kCustom, calls=%fused_computation.15 | custom fusion | bytes 4194306 | tf_op jit(solution)/shard_map/scatter | solution.py:82
  84.7 0.0 all-to-all-done.1
  84.7 7.6 %all-to-all-start.2 = ((bf16[32,512,128]{2,1,0:T(8,128)(2,1)}), bf16[32,512,128]{2,1,0:T(8,128)(2,1)}, u32[]{:S(2)}, u32[]{:S(2)}) async-start(bf16[32,512,128]{2,1,0:T(8,128)(2,1)} %bitcast.65), calls=%async_computation.2 | async-start | bytes 8388608 | tf_op jit(solution)/shard_map/all_to_all | solution.py:87
  92.3 0.0 copy-start.8
  92.3 0.2 reduce-scatter.4.cloned.1.call-start
  92.5 0.0 copy-done.5
  92.5 0.3 convolution_bitcast_fusion
  92.9 1.3 copy.17
  94.2 0.0 reduce-scatter.4.cloned.1.call-update
  94.2 0.0 copy-done.8
  94.2 6.2 %gather_fusion = f32[1024]{0:T(1024)S(1)} fusion(f32[4096]{0:T(1024)S(1)} %bitcast.62, s32[1024]{0:T(1024)S(1)} %broadcast_clamp_fusion), kind=kCustom, calls=%fused_computation.1 | custom fusion | bytes 12288 | tf_op jit(solution)/shard_map/gather | solution.py:95
  100.4 0.2 reduce.2
  100.6 82.0 %reduce-scatter.4.cloned.1.call-done = f32[32,256]{1,0:T(8,128)} async-done(((f32[1024,256]{1,0:T(8,128)}), f32[32,256]{1,0:T(8,128)}) %reduce-scatter.4.cloned.1.call-update) | async-done | bytes 32784
  182.6 0.9 copy.18
  183.5 0.7 copy.16
  184.2 0.0 all-to-all-done.2
  184.2 18.0 %while.11 = (s32[]{:T(128)}, f32[1024,128]{1,0:T(8,128)S(1)}, s32[4,4096]{1,0:T(4,128)S(1)}, bf16[4,4096,128]{2,1,0:T(8,128)(2,1)}, s32[]{:T(128)}, /*index=5*/s32[]{:T(128)}) while((s32[]{:T(128)}, f32[1024,128]{1,0:T(8,128)S(1)}, s32[4,4096]{1,0:T(4,128)S(1)}, bf16[4,4096,128]{2,1,0:T(8,128)(2,1)}, s32[]{:T(128)}, ...), condition=%wide.region_5.6_spmd.clone, body=%wide.region_4.5_spmd.clone.sunk | while | flops 1078198272 | bytes 2146899 | solution.py:48
  184.2 4.4 %fusion.41 = f32[1024,128]{1,0:T(8,128)S(1)} fusion(s32[4096]{0:T(1024)S(1)} %bitcast.70, bf16[4,4096,128]{2,1,0:T(8,128)(2,1)} %get-tuple-element.107, s32[]{:T(128)} %get-tuple-element.98, f32[1024,128]{1,0:T(8,128)S(1)} %get-tuple-element.99, pred[]{:T(512)S(6)} %compare.3), kind=kOutput, calls=%fused_computation.10.clone.1 | convolution fusion | flops 1078198272 | bytes 2114049 | tf_op jit(solution)/shard_map/while/body/eval_jaxpr/dot_general | solution.py:45
  188.7 4.5 %fusion.41 = f32[1024,128]{1,0:T(8,128)S(1)} fusion(s32[4096]{0:T(1024)S(1)} %bitcast.70, bf16[4,4096,128]{2,1,0:T(8,128)(2,1)} %get-tuple-element.107, s32[]{:T(128)} %get-tuple-element.98, f32[1024,128]{1,0:T(8,128)S(1)} %get-tuple-element.99, pred[]{:T(512)S(6)} %compare.3), kind=kOutput, calls=%fused_computation.10.clone.1 | convolution fusion | flops 1078198272 | bytes 2114049 | tf_op jit(solution)/shard_map/while/body/eval_jaxpr/dot_general | solution.py:45
  193.2 4.4 %fusion.41 = f32[1024,128]{1,0:T(8,128)S(1)} fusion(s32[4096]{0:T(1024)S(1)} %bitcast.70, bf16[4,4096,128]{2,1,0:T(8,128)(2,1)} %get-tuple-element.107, s32[]{:T(128)} %get-tuple-element.98, f32[1024,128]{1,0:T(8,128)S(1)} %get-tuple-element.99, pred[]{:T(512)S(6)} %compare.3), kind=kOutput, calls=%fused_computation.10.clone.1 | convolution fusion | flops 1078198272 | bytes 2114049 | tf_op jit(solution)/shard_map/while/body/eval_jaxpr/dot_general | solution.py:45
  197.7 4.5 %fusion.41 = f32[1024,128]{1,0:T(8,128)S(1)} fusion(s32[4096]{0:T(1024)S(1)} %bitcast.70, bf16[4,4096,128]{2,1,0:T(8,128)(2,1)} %get-tuple-element.107, s32[]{:T(128)} %get-tuple-element.98, f32[1024,128]{1,0:T(8,128)S(1)} %get-tuple-element.99, pred[]{:T(512)S(6)} %compare.3), kind=kOutput, calls=%fused_computation.10.clone.1 | convolution fusion | flops 1078198272 | bytes 2114049 | tf_op jit(solution)/shard_map/while/body/eval_jaxpr/dot_general | solution.py:45
  202.2 0.2 multiply_reduce_fusion
  202.4 0.0 copy-start.3
  202.4 4.3 %scatter_fusion = f32[4096]{0:T(1024)S(1)} fusion(f32[4096]{0:T(1024)S(1)} %bitcast.63, s32[1024]{0:T(1024)S(1)} %bitcast.75, f32[1024]{0:T(1024)S(1)} %get-tuple-element.66), kind=kCustom, calls=%fused_computation.5 | custom fusion | bytes 16384 | tf_op jit(solution)/shard_map/scatter | solution.py:100
  206.8 0.0 copy-start.1
  206.8 7.1 %scatter_custom_fusion.2 = f32[4096,128]{1,0:T(8,128)S(1)} fusion(f32[4096,128]{1,0:T(8,128)S(1)} %bitcast.67, s32[1024]{0:T(1024)S(1)} %bitcast.76, f32[1024,128]{1,0:T(8,128)S(1)} %get-tuple-element.30, f32[1024]{0:T(1024)S(1)} %get-tuple-element.65, f32[]{:T(128)} %constant.12.clone.1, s32[1024]{0:T(1024)S(1)} %broadcast_clamp_fusion), kind=kCustom, calls=%fused_computation.28 | custom fusion | flops 393216 | bytes 4726788 | tf_op jit(solution)/shard_map/scatter | solution.py:99
  213.9 0.0 copy-start.2
  213.9 1.3 copy-done.2
  (16 shorter events, 0.2 us)
Async XLA Ops:
  7.2 52.4 %copy-start = (bf16[1,1024,256]{2,1,0:T(8,128)(2,1)S(1)}, bf16[1,1024,256]{2,1,0:T(8,128)(2,1)}, u32[]{:S(2)}) copy-start(bf16[1,1024,256]{2,1,0:T(8,128)(2,1)} %param.12) | copy-start | bytes 1572868
  8.0 0.9 copy-start.7
  8.0 10.7 %copy-start.6 = (s32[1,1,8192,1]{2,3,1,0:T(1,128)S(1)}, s32[1,1,8192,1]{2,3,1,0:T(1,128)}, u32[]{:S(2)}) copy-start(s32[1,1,8192,1]{2,3,1,0:T(1,128)} %param.13) | copy-start | bytes 98308
  9.5 50.0 %copy-start.4 = (bf16[1,1,256,1024]{3,2,1,0:T(8,128)(2,1)S(1)}, bf16[1,1,256,1024]{3,2,1,0:T(8,128)(2,1)}, u32[]{:S(2)}) copy-start(bf16[1,1,256,1024]{3,2,1,0:T(8,128)(2,1)} %param.11) | copy-start | bytes 1572868
  9.5 41.9 %all-to-all-start = ((bf16[32,8,256]{2,0,1:T(8,128)(2,1)}), bf16[32,8,256]{2,0,1:T(8,128)(2,1)S(1)}, u32[]{:S(2)}, u32[]{:S(2)}) async-start(bf16[32,8,256]{2,0,1:T(8,128)(2,1)} %copy.15), calls=%async_computation | async-start | bytes 262144 | tf_op jit(solution)/shard_map/all_to_all | solution.py:54
  51.4 33.3 %all-to-all-start.1 = ((s32[32,1,512]{2,1,0:T(1,128)}), s32[32,1,512]{2,1,0:T(1,128)S(1)}, u32[]{:S(2)}, u32[]{:S(2)}) async-start(s32[32,1,512]{2,1,0:T(1,128)} %bitcast.16), calls=%async_computation.1 | async-start | bytes 131072 | tf_op jit(solution)/shard_map/all_to_all | solution.py:88
  84.7 7.8 %copy-start.5 = (bf16[1,1,256,1024]{3,2,1,0:T(8,128)(2,1)S(1)}, bf16[1,1,256,1024]{3,2,1,0:T(8,128)(2,1)}, u32[]{:S(2)}) copy-start(bf16[1,1,256,1024]{3,2,1,0:T(8,128)(2,1)} %param.11) | copy-start | bytes 1572868
  84.7 99.4 %all-to-all-start.2 = ((bf16[32,512,128]{2,1,0:T(8,128)(2,1)}), bf16[32,512,128]{2,1,0:T(8,128)(2,1)}, u32[]{:S(2)}, u32[]{:S(2)}) async-start(bf16[32,512,128]{2,1,0:T(8,128)(2,1)} %bitcast.65), calls=%async_computation.2 | async-start | bytes 8388608 | tf_op jit(solution)/shard_map/all_to_all | solution.py:87
  92.3 1.9 copy-start.8
  92.3 90.3 %reduce-scatter.4.cloned.1.call-start = ((), (), s32[]{:S(2)}) async-start(), calls=%async_computation.4 | async-start | bytes 1081344
  202.4 4.4 %copy-start.3 = (f32[1,4096,128]{2,1,0:T(8,128)S(1)}, f32[1,4096,128]{2,1,0:T(8,128)}, u32[]{:S(2)}) copy-start(f32[1,4096,128]{2,1,0:T(8,128)} %param.16) | copy-start | bytes 6291460
  206.8 7.1 %copy-start.1 = (f32[4096]{0:T(1024)}, f32[4096]{0:T(1024)S(1)}, u32[]{:S(2)}) copy-start(f32[4096]{0:T(1024)S(1)} %scatter_fusion) | copy-start | bytes 49156
  213.9 1.3 copy-start.2
Sparse Core Ops, SparseCore 0:
  97.5 85.0 reduce-scatter.3
where the time goes:
time: 223 us; the launch traced here: 222 us
  waiting for transfers between devices  82 us (37%)
  local copies, waits for them, and re-layouts  73.5 us (33%)
  starting transfers between devices  25 us (11%)
  matrix products  19.2 us (9%)
  between operations  14.3 us (6%)
  other arithmetic  7.91 us (4%)
    unnamed x2, waiting for transfers between devices  82 us
    scatter x1, local copies, waits for them, and re-layouts, shards(): jnp.full((slot_total,), -1, jnp.int32).at[dest].set(slots_own, mode='drop')  31.2 us
    scatter x1, local copies, waits for them, and re-layouts, shards(): jnp.zeros((slot_total, E), jnp.bfloat16).at[dest]  23.6 us
    dot_general x4, matrix products, add_block(): jnp.dot(onehot, block_pair[0], preferred_element_type=jnp.float32)  17.8 us
    all_to_all x1, starting transfers between devices, shards(): lax.all_to_all(grad_out, 'tower', split_axis=1, concat_axis=0, tiled=True)  9.13 us
    all_to_all x1, starting transfers between devices, shards(): lax.all_to_all(row_slots, 'dev', split_axis=0, concat_axis=0, tiled=True)  8.04 us
    all_to_all x1, starting transfers between devices, shards(): lax.all_to_all(send_values, 'dev', split_axis=0, concat_axis=0, tiled=True)  7.57 us
    scatter x1, other arithmetic, shards(): new_table = table_local.at[local_rows].set(updated)  7.09 us
  transfers between devices with their start and end apart: 4, of which 1 were waited for; matrix products, arithmetic and copies ran while one was open for 30% of the time, Pallas kernels for 0%

commit v1 on v0

--- a/solution.py
+++ b/solution.py
@@ -3,15 +3,20 @@
 import jax
 import jax.numpy as jnp
 from jax import lax
+from jax.experimental import pallas as pl
+from jax.experimental.pallas import tpu as pltpu
 from jax.sharding import PartitionSpec as P
 
 E = 128
 HOT = 4
+CAP = 512
 
 
 learn_rate = 0.1
 epsilon = 1e-06
 highest = lax.Precision.HIGHEST
+f32 = jnp.float32
+bf16 = jnp.bfloat16
 
 
 def count_before(matches):
@@ -49,63 +54,142 @@
     return result
 
 
+def dense_pack_kernel(dest_ref, grad_ref, pooled_ref, w_ref, packed_ref, gw_ref, bag_ref, rows_ref):
+    total = rows_ref.shape[0]
+    step = 512
+
+    @pl.loop(0, total // step)
+    def _(i):
+        rows_ref[pl.ds(pl.multiple_of(i * step, step), step), :] = jnp.zeros((step, E), f32)
+
+    preact = jnp.dot(pooled_ref[...], w_ref[...], preferred_element_type=f32)
+    sigma = 1.0 / (1.0 + jnp.exp(-preact))
+    grad_pre = (grad_ref[...].astype(f32) * sigma * (1.0 + preact * (1.0 - sigma))).astype(bf16)
+    gw_ref[...] = lax.dot_general(
+        pooled_ref[...], grad_pre, (((0,), (0,)), ((), ())), preferred_element_type=f32
+    )
+    feats, group, _ = bag_ref.shape
+    for f in range(feats):
+        bag_ref[f] = (
+            lax.dot_general(
+                grad_pre,
+                w_ref[f * E : (f + 1) * E, :],
+                (((1,), (1,)), ((), ())),
+                preferred_element_type=f32,
+            )
+            .astype(bf16)
+            .astype(f32)
+        )
+
+    @pl.loop(0, group)
+    def _(g):
+        for f in range(feats):
+            row = bag_ref[f, pl.ds(g, 1), :]
+            for k in range(HOT):
+                d = dest_ref[g * (feats * HOT) + f * HOT + k]
+                rows_ref[pl.ds(d, 1), :] = row
+
+    @pl.loop(0, total // step)
+    def _(i):
+        at = pl.ds(pl.multiple_of(i * step, step), step)
+        packed_ref[at, :] = rows_ref[at, :].astype(bf16)
+
+
+def dense_pack(dest, grad_tower, pooled_rows, weight, slot_total):
+    vmem = pl.BlockSpec(memory_space=pltpu.VMEM)
+    group, depth = pooled_rows.shape
+    return pl.pallas_call(
+        dense_pack_kernel,
+        out_shape=(
+            jax.ShapeDtypeStruct((slot_total, E), bf16),
+            jax.ShapeDtypeStruct(weight.shape, f32),
+        ),
+        in_specs=[pl.BlockSpec(memory_space=pltpu.SMEM), vmem, vmem, vmem],
+        out_specs=(vmem, vmem),
+        scratch_shapes=[
+            pltpu.VMEM((depth // E, group, E), f32),
+            pltpu.VMEM((slot_total, E), f32),
+        ],
+        name="dense_pack",
+    )(dest, grad_tower, pooled_rows, weight)
+
+
+def update_kernel(rows_ref, col_ref, grad_ref, table_ref, accum_ref, out_ref, accum_out, upd_ref):
+    row_grad = grad_ref[...]
+    count = row_grad.shape[0]
+    sq_mean = jnp.mean(row_grad * row_grad, axis=1, keepdims=True)
+    col = col_ref[...]
+    lanes = lax.broadcasted_iota(jnp.int32, (count, E), 1)
+    blocks = accum_ref.shape[0]
+    high = (lax.broadcasted_iota(jnp.int32, (count, blocks), 1) == col // E).astype(f32)
+    low = (lanes == lax.rem(col, E)).astype(f32)
+    spread = jnp.dot(high, accum_ref[...], precision=highest, preferred_element_type=f32)
+    accum_touched = jnp.sum(spread * low, axis=1, keepdims=True) + sq_mean
+    accum_out[...] = accum_ref[...] + lax.dot_general(
+        high, low * sq_mean, (((0,), (0,)), ((), ())), precision=highest, preferred_element_type=f32
+    )
+    upd_ref[...] = learn_rate * row_grad / jnp.sqrt(accum_touched + epsilon)
+    out_ref[...] = table_ref[...]
+
+    @pl.loop(0, count // 8)
+    def _(i):
+        for k in range(8):
+            u = i * 8 + k
+            r = rows_ref[u]
+            out_ref[pl.ds(r, 1), :] = table_ref[pl.ds(r, 1), :] - upd_ref[pl.ds(u, 1), :]
+
+
+def update(touched, row_grad, table, accum):
+    vmem = pl.BlockSpec(memory_space=pltpu.VMEM)
+    new_table, new_accum = pl.pallas_call(
+        update_kernel,
+        out_shape=(
+            jax.ShapeDtypeStruct(table.shape, f32),
+            jax.ShapeDtypeStruct((accum.shape[0] // E, E), f32),
+        ),
+        in_specs=[pl.BlockSpec(memory_space=pltpu.SMEM), vmem, vmem, vmem, vmem],
+        out_specs=(vmem, vmem),
+        scratch_shapes=[pltpu.VMEM(row_grad.shape, f32)],
+        name="row_update",
+    )(touched, touched[:, None], row_grad, table, accum.reshape(-1, E))
+    return new_table, new_accum.reshape(-1)
+
+
 def shards(grad_out, pooled, compress_w, owner_ids, slot_ids, touched, table, accum):
     owners = lax.axis_size("dev")
     moved = lax.all_to_all(grad_out, "tower", split_axis=1, concat_axis=0, tiled=True)
     grad_tower = moved[:, 0, :]
     pooled_rows = pooled[0, 0]
     weight = compress_w[0]
-    preact = jnp.dot(pooled_rows, weight, preferred_element_type=jnp.float32)
-    sigma = jax.nn.sigmoid(preact)
-    grad_pre = (grad_tower.astype(jnp.float32) * sigma * (1.0 + preact * (1.0 - sigma))).astype(
-        jnp.bfloat16
-    )
     occurrences = owner_ids.shape[2]
-    capacity = 2 * occurrences // owners
     touch_count = touched.shape[2]
-    slot_total = owners * capacity
-    bag_rows = (
-        lax.dot_general(
-            grad_pre, weight, (((1,), (1,)), ((), ())), preferred_element_type=jnp.float32
-        )
-        .astype(jnp.bfloat16)
-        .reshape(-1, E)
-    )
-    occ_values = jnp.repeat(bag_rows, HOT, axis=0)
+    slot_total = owners * CAP
     targets_own = owner_ids[0, 0, :, 0]
     slots_own = slot_ids[0, 0]
     owner_iota = lax.broadcasted_iota(jnp.int32, (owners, occurrences), 0)
     matches = targets_own[None, :] == owner_iota
     ranks = count_before(matches)
     own_rank = jnp.sum(jnp.where(matches, ranks, 0), axis=0)
-    dest = targets_own * capacity + own_rank
-    send_values = jnp.zeros((slot_total, E), jnp.bfloat16).at[dest].set(occ_values, mode="drop")
-    row_slots = jnp.full((slot_total,), -1, jnp.int32).at[dest].set(slots_own, mode="drop")
-    send_values = send_values.reshape(owners, capacity, E)
-    row_slots = row_slots.reshape(owners, capacity)
+    dest = targets_own * CAP + own_rank
+    parts = jnp.concatenate(
+        [
+            jnp.where(matches, slots_own[None, :] // 32, 0).astype(bf16),
+            jnp.where(matches, slots_own[None, :] % 32, 0).astype(bf16),
+        ]
+    )
+    at_rank = (own_rank[:, None] == lax.broadcasted_iota(jnp.int32, (occurrences, CAP), 1)).astype(bf16)
+    packed_slots = jnp.dot(parts, at_rank, preferred_element_type=f32)
+    row_slots = (packed_slots[:owners] * 32 + packed_slots[owners:]).astype(jnp.int32)
+
+    send_values, grad_weight = dense_pack(dest, grad_tower, pooled_rows, weight, slot_total)
+    send_values = send_values.reshape(owners, CAP, E)
     recv_values, recv_slots = (
         lax.all_to_all(send_values, "dev", split_axis=0, concat_axis=0, tiled=True),
         lax.all_to_all(row_slots, "dev", split_axis=0, concat_axis=0, tiled=True),
     )
     row_grad = accumulate(recv_values.reshape(-1, E), recv_slots.reshape(-1), touch_count)
-    sq_mean = jnp.mean(row_grad * row_grad, axis=1)
-    local_rows = touched[0, 0]
-    accum_local = accum[0]
-    table_local = table[0]
-    accum_touched = accum_local[local_rows] + sq_mean
-    updated = (
-        table_local[local_rows] - learn_rate * row_grad / jnp.sqrt(accum_touched + epsilon)[:, None]
-    )
-    new_table = table_local.at[local_rows].set(updated)
-    new_accum = accum_local.at[local_rows].set(accum_touched)
-    grad_weight = lax.psum_scatter(
-        lax.dot_general(
-            pooled_rows, grad_pre, (((0,), (0,)), ((), ())), preferred_element_type=jnp.float32
-        ),
-        "dev",
-        scatter_dimension=0,
-        tiled=True,
-    )
+    new_table, new_accum = update(touched[0, 0], row_grad, table[0], accum[0])
+    grad_weight = lax.psum_scatter(grad_weight, "dev", scatter_dimension=0, tiled=True)
     return (grad_weight[None], new_table[None], new_accum[None])
 
 

time: 223 us -> 154 us (0.69)
  local copies, waits for them, and re-layouts: 73.5 us -> 4.06 us
  Pallas kernels: 0 us -> 19.8 us
  waiting for transfers between devices: 82 us -> 64 us
  other arithmetic: 7.91 us -> 3.62 us
  matrix products: 19.2 us -> 21.9 us
    unnamed x2 -> x1, waiting for transfers between devices: 82 us -> 0.02 us
    scatter x3 -> x0, local copies, waits for them, and re-layouts: 59.2 us -> none  [the longest x1 31.2 us: shards(): jnp.full((slot_total,), -1, jnp.int32).at[dest].set(slots_own, mode='drop')]
    all_to_all x1, waiting for transfers between devices: 0.01 us -> 50.8 us  [shards(): lax.all_to_all(send_values, 'dev', split_axis=0, concat_axis=0, tiled=True)]
    pallas_call x0 -> x2, Pallas kernels: none -> 19.8 us  [the longest x1 13.6 us: dense_pack(): pl.pallas_call(dense_pack_kernel, out_shape=(jax.ShapeDtypeStruct((slot_t...]
    reduce_scatter x0 -> x1, waiting for transfers between devices: none -> 13.2 us  [shards(): lax.psum_scatter(grad_weight, 'dev', scatter_dimension=0, tiled=True)]
    scatter x1 -> x0, other arithmetic: 7.09 us -> none  [shards(): new_table = table_local.at[local_rows].set(updated)]
    gather x1 -> x0, local copies, waits for them, and re-layouts: 6.15 us -> none  [shards(): accum_touched = accum_local[local_rows] + sq_mean]
    unnamed x23 -> x7, local copies, waits for them, and re-layouts: 6.57 us -> 1.6 us
  transfers between devices with their start and end apart: 4 -> 4, of which waited for: 1 -> 2; matrix products, arithmetic and copies ran while one was open for 30% -> 18% of each run, Pallas kernels for 0% -> 13%
where the time goes in v1:
time: 154 us; the launch traced here: 153 us
  waiting for transfers between devices  64 us (42%)
  starting transfers between devices  25.5 us (17%)
  matrix products  21.9 us (14%)
  Pallas kernels  19.8 us (13%)
  between operations  14.1 us (9%)
  local copies, waits for them, and re-layouts  4.06 us (3%)
  other arithmetic  3.62 us (2%)
    all_to_all x1, waiting for transfers between devices, shards(): lax.all_to_all(send_values, 'dev', split_axis=0, concat_axis=0, tiled=True)  50.8 us
    dot_general x4, matrix products, add_block(): jnp.dot(onehot, block_pair[0], preferred_element_type=jnp.float32)  17.8 us
    pallas_call x1, Pallas kernels, dense_pack(): pl.pallas_call(dense_pack_kernel, out_shape=(jax.ShapeDtypeStruct((slot_t...  13.6 us
    reduce_scatter x1, waiting for transfers between devices, shards(): lax.psum_scatter(grad_weight, 'dev', scatter_dimension=0, tiled=True)  13.2 us
    all_to_all x1, starting transfers between devices, shards(): lax.all_to_all(grad_out, 'tower', split_axis=1, concat_axis=0, tiled=True)  9 us
    all_to_all x1, starting transfers between devices, shards(): lax.all_to_all(row_slots, 'dev', split_axis=0, concat_axis=0, tiled=True)  8.85 us
    all_to_all x1, starting transfers between devices, shards(): lax.all_to_all(send_values, 'dev', split_axis=0, concat_axis=0, tiled=True)  7.57 us
    pallas_call x1, Pallas kernels, update(): pl.pallas_call(update_kernel, out_shape=(jax.ShapeDtypeStruct(table.shape...  6.22 us
  transfers between devices with their start and end apart: 4, of which 2 were waited for; matrix products, arithmetic and copies ran while one was open for 18% of the time, Pallas kernels for 13%

profile of v1, /device:TPU:1, one launch (start us, length us, event | category | flops | bytes accessed | tf_op | source)
XLA Modules:
  0.0 153.1 jit_solution(7409213392782401374)
XLA Ops:
  7.2 1.6 %copy.14 = bf16[32,8,256]{2,0,1:T(8,128)(2,1)} copy(bf16[32,8,256]{2,1,0:T(8,128)(2,1)} %param.10) | data formatting | bytes 262144 | tf_op args[0]
  8.7 9.0 %all-to-all-start = ((bf16[32,8,256]{2,0,1:T(8,128)(2,1)}), bf16[32,8,256]{2,0,1:T(8,128)(2,1)S(1)}, u32[]{:S(2)}, u32[]{:S(2)}) async-start(bf16[32,8,256]{2,0,1:T(8,128)(2,1)} %copy.14), calls=%async_computation | async-start | bytes 262144 | tf_op jit(solution)/shard_map/all_to_all | solution.py:160
  17.8 1.1 fusion.13
  18.8 0.6 slice_reduce_fusion
  19.5 0.1 fusion.19
  19.6 1.1 select_reduce_fusion
  20.7 0.8 add_select_fusion.1
  21.5 0.9 select_convert_fusion.1
  22.4 0.0 copy-start
  22.4 2.9 %fusion.8 = f32[64,512]{1,0:T(8,128)S(1)} fusion(s32[8192]{0:T(1024)S(1)} %bitcast.45, bf16[32,8192]{1,0:T(8,128)(2,1)S(1)} %get-tuple-element.65, bf16[32,8192]{1,0:T(8,128)(2,1)S(1)} %get-tuple-element.64), kind=kOutput, calls=%fused_computation.10 | convolution fusion | flops 543162368 | bytes 1212416 | tf_op jit(solution)/shard_map/dot_general | solution.py:181
  25.3 0.7 copy.15
  26.0 0.0 all-to-all-done
  26.0 0.0 copy-start.1
  26.0 8.9 %all-to-all-start.1 = ((s32[32,1,512]{2,1,0:T(1,128)}), s32[32,1,512]{2,1,0:T(1,128)S(1)}, u32[]{:S(2)}, u32[]{:S(2)}) async-start(s32[32,1,512]{2,1,0:T(1,128)} %copy.15), calls=%async_computation.2 | async-start | bytes 131072 | tf_op jit(solution)/shard_map/all_to_all | solution.py:188
  34.9 0.0 copy-done
  34.9 0.6 multiply_add_fusion.dest_ref
  35.5 0.0 copy-done.1
  35.5 13.6 %dense_pack.1 = (bf16[16384,128]{1,0:T(8,128)(2,1)}, f32[1024,256]{1,0:T(8,128)}) custom-call(s32[8192]{0:T(1024)} %multiply_add_fusion.dest_ref, bf16[256,256]{1,0:T(8,128)(2,1)} %bitcast.43, bf16[256,1024]{1,0:T(8,128)(2,1)} %bitcast.41, bf16[1024,256]{1,0:T(8,128)(2,1)} %bitcast.42), custom_call_target="tpu_custom_call" | custom-call | tf_op jit(solution)/shard_map/dense_pack/pallas_call | solution.py:101
  49.2 0.0 all-to-all-done.1
  49.2 0.0 copy-start.2
  49.2 7.6 %all-to-all-start.2 = ((bf16[32,512,128]{2,1,0:T(8,128)(2,1)}), bf16[32,512,128]{2,1,0:T(8,128)(2,1)}, u32[]{:S(2)}, u32[]{:S(2)}) async-start(bf16[32,512,128]{2,1,0:T(8,128)(2,1)} %bitcast.35), calls=%async_computation.3 | async-start | bytes 8388608 | tf_op jit(solution)/shard_map/all_to_all | solution.py:187
  56.7 0.0 reduce-scatter.2.cloned.1.call-start
  56.8 0.0 copy-done.2
  56.8 1.0 copy.16.col_ref
  57.8 0.2 reduce.2
  58.0 0.0 reduce-scatter.2.cloned.1.call-update
  58.1 50.8 %all-to-all-done.2 = bf16[32,512,128]{2,1,0:T(8,128)(2,1)} async-done(((bf16[32,512,128]{2,1,0:T(8,128)(2,1)}), bf16[32,512,128]{2,1,0:T(8,128)(2,1)}, u32[]{:S(2)}, u32[]{:S(2)}) %all-to-all-start.2) | async-done | bytes 4194336 | tf_op jit(solution)/shard_map/all_to_all | solution.py:187
  108.9 18.0 %while.11 = (s32[]{:T(128)}, f32[1024,128]{1,0:T(8,128)S(1)}, s32[4,4096]{1,0:T(4,128)S(1)}, bf16[4,4096,128]{2,1,0:T(8,128)(2,1)}, s32[]{:T(128)}, /*index=5*/s32[]{:T(128)}) while((s32[]{:T(128)}, f32[1024,128]{1,0:T(8,128)S(1)}, s32[4,4096]{1,0:T(4,128)S(1)}, bf16[4,4096,128]{2,1,0:T(8,128)(2,1)}, s32[]{:T(128)}, ...), condition=%wide.region_3.4_spmd.clone, body=%wide.region_2.3_spmd.clone.sunk | while | flops 1078198272 | bytes 2146899 | solution.py:53
  108.9 4.4 %fusion.27 = f32[1024,128]{1,0:T(8,128)S(1)} fusion(s32[4096]{0:T(1024)S(1)} %bitcast.44, bf16[4,4096,128]{2,1,0:T(8,128)(2,1)} %get-tuple-element.108, s32[]{:T(128)} %get-tuple-element.99, f32[1024,128]{1,0:T(8,128)S(1)} %get-tuple-element.100, pred[]{:T(512)S(6)} %compare.16), kind=kOutput, calls=%fused_computation.4.clone.1 | convolution fusion | flops 1078198272 | bytes 2114049 | tf_op jit(solution)/shard_map/while/body/eval_jaxpr/dot_general | solution.py:50
  113.4 4.5 %fusion.27 = f32[1024,128]{1,0:T(8,128)S(1)} fusion(s32[4096]{0:T(1024)S(1)} %bitcast.44, bf16[4,4096,128]{2,1,0:T(8,128)(2,1)} %get-tuple-element.108, s32[]{:T(128)} %get-tuple-element.99, f32[1024,128]{1,0:T(8,128)S(1)} %get-tuple-element.100, pred[]{:T(512)S(6)} %compare.16), kind=kOutput, calls=%fused_computation.4.clone.1 | convolution fusion | flops 1078198272 | bytes 2114049 | tf_op jit(solution)/shard_map/while/body/eval_jaxpr/dot_general | solution.py:50
  117.9 4.4 %fusion.27 = f32[1024,128]{1,0:T(8,128)S(1)} fusion(s32[4096]{0:T(1024)S(1)} %bitcast.44, bf16[4,4096,128]{2,1,0:T(8,128)(2,1)} %get-tuple-element.108, s32[]{:T(128)} %get-tuple-element.99, f32[1024,128]{1,0:T(8,128)S(1)} %get-tuple-element.100, pred[]{:T(512)S(6)} %compare.16), kind=kOutput, calls=%fused_computation.4.clone.1 | convolution fusion | flops 1078198272 | bytes 2114049 | tf_op jit(solution)/shard_map/while/body/eval_jaxpr/dot_general | solution.py:50
  122.4 4.5 %fusion.27 = f32[1024,128]{1,0:T(8,128)S(1)} fusion(s32[4096]{0:T(1024)S(1)} %bitcast.44, bf16[4,4096,128]{2,1,0:T(8,128)(2,1)} %get-tuple-element.108, s32[]{:T(128)} %get-tuple-element.99, f32[1024,128]{1,0:T(8,128)S(1)} %get-tuple-element.100, pred[]{:T(512)S(6)} %compare.16), kind=kOutput, calls=%fused_computation.4.clone.1 | convolution fusion | flops 1078198272 | bytes 2114049 | tf_op jit(solution)/shard_map/while/body/eval_jaxpr/dot_general | solution.py:50
  126.9 6.2 %row_update.1 = (f32[4096,128]{1,0:T(8,128)}, f32[32,128]{1,0:T(8,128)}) custom-call(s32[1024]{0:T(1024)} %bitcast.48, s32[1024,1]{1,0:T(8,128)} %copy.16.col_ref, f32[1024,128]{1,0:T(8,128)S(1)} %get-tuple-element.36.grad_ref, f32[4096,128]{1,0:T(8,128)} %bitcast.36, f32[32,128]{1,0:T(8,128)} %bitcast.47), custom_call_target="tpu_custom_call" | custom-call | tf_op jit(solution)/shard_map/row_update/pallas_call | solution.py:144
  133.1 13.2 %reduce-scatter.2.cloned.1.call-done = f32[32,256]{1,0:T(8,128)} async-done(((f32[1024,256]{1,0:T(8,128)}), f32[32,256]{1,0:T(8,128)}) %reduce-scatter.2.cloned.1.call-update) | async-done | bytes 32784 | tf_op jit(solution)/shard_map/reduce_scatter | solution.py:192
  (7 shorter events, 0.1 us)
Async XLA Ops:
  8.7 17.3 %all-to-all-start = ((bf16[32,8,256]{2,0,1:T(8,128)(2,1)}), bf16[32,8,256]{2,0,1:T(8,128)(2,1)S(1)}, u32[]{:S(2)}, u32[]{:S(2)}) async-start(bf16[32,8,256]{2,0,1:T(8,128)(2,1)} %copy.14), calls=%async_computation | async-start | bytes 262144 | tf_op jit(solution)/shard_map/all_to_all | solution.py:160
  22.4 12.5 %copy-start = (s32[1,1,8192,1]{2,3,1,0:T(1,128)S(1)}, s32[1,1,8192,1]{2,3,1,0:T(1,128)}, u32[]{:S(2)}) copy-start(s32[1,1,8192,1]{2,3,1,0:T(1,128)} %param.13) | copy-start | bytes 98308
  26.0 9.5 %copy-start.1 = (bf16[32,8,256]{2,0,1:T(8,128)(2,1)}, bf16[32,8,256]{2,0,1:T(8,128)(2,1)S(1)}, u32[]{:S(2)}) copy-start(bf16[32,8,256]{2,0,1:T(8,128)(2,1)S(1)} %all-to-all-done) | copy-start | bytes 393220
  26.0 23.1 %all-to-all-start.1 = ((s32[32,1,512]{2,1,0:T(1,128)}), s32[32,1,512]{2,1,0:T(1,128)S(1)}, u32[]{:S(2)}, u32[]{:S(2)}) async-start(s32[32,1,512]{2,1,0:T(1,128)} %copy.15), calls=%async_computation.2 | async-start | bytes 131072 | tf_op jit(solution)/shard_map/all_to_all | solution.py:188
  49.2 7.6 %copy-start.2 = (s32[1,1,1024]{2,1,0:T(1,128)S(1)}, s32[1,1,1024]{2,1,0:T(1,128)}, u32[]{:S(2)}) copy-start(s32[1,1,1024]{2,1,0:T(1,128)} %param.15) | copy-start | bytes 12292
  49.2 59.7 %all-to-all-start.2 = ((bf16[32,512,128]{2,1,0:T(8,128)(2,1)}), bf16[32,512,128]{2,1,0:T(8,128)(2,1)}, u32[]{:S(2)}, u32[]{:S(2)}) async-start(bf16[32,512,128]{2,1,0:T(8,128)(2,1)} %bitcast.35), calls=%async_computation.3 | async-start | bytes 8388608 | tf_op jit(solution)/shard_map/all_to_all | solution.py:187
  56.7 89.5 %reduce-scatter.2.cloned.1.call-start = ((), (), s32[]{:S(2)}) async-start(), calls=%async_computation.4 | async-start | bytes 1081344 | tf_op jit(solution)/shard_map/reduce_scatter | solution.py:192
Sparse Core Ops, SparseCore 0:
  61.9 84.2 reduce-scatter.1

commit v2 on v1

--- a/solution.py
+++ b/solution.py
@@ -15,6 +15,7 @@
 learn_rate = 0.1
 epsilon = 1e-06
 highest = lax.Precision.HIGHEST
+MESH = pl.DeviceIdType.MESH
 f32 = jnp.float32
 bf16 = jnp.bfloat16
 
@@ -35,23 +36,6 @@
     offsets = jnp.dot(totals, strict, precision=highest, preferred_element_type=jnp.float32)
     ranks = within + offsets[:, :, None]
     return ranks.reshape(row_total, length).astype(jnp.int32) - 1
-
-
-def accumulate(values, slot_flat, touch_count):
-    total_rows = values.shape[0]
-    block_size = math.gcd(total_rows, 4096)
-    block_count = total_rows // block_size
-    value_blocks = values.reshape(block_count, block_size, values.shape[1])
-    slot_blocks = slot_flat.reshape(block_count, block_size)
-    targets = lax.broadcasted_iota(jnp.int32, (touch_count, block_size), 0)
-
-    def add_block(totals, block_pair):
-        onehot = (block_pair[1][None, :] == targets).astype(jnp.bfloat16)
-        return (totals + jnp.dot(onehot, block_pair[0], preferred_element_type=jnp.float32), None)
-
-    start_sum = jnp.zeros((touch_count, values.shape[1]), jnp.float32)
-    result, unused = lax.scan(add_block, start_sum, (value_blocks, slot_blocks))
-    return result
 
 
 def dense_pack_kernel(dest_ref, grad_ref, pooled_ref, w_ref, packed_ref, gw_ref, bag_ref, rows_ref):
@@ -155,6 +139,273 @@
     return new_table, new_accum.reshape(-1)
 
 
+SIDE = 4
+HALF = 512
+GW_HALF = 16
+
+
+def reduce_kernel(
+    packed_ref, slots_ref, gw_ref, out_ref, gw_out,
+    pk_recv, sl_recv, gw_recv, s1, r1, s2, r2, own, s3, r3, s4, r4,
+    gs1, gr1, gs2, gr2, gown, gs3, gr3, gs4, gr4, send_sem, recv_sem,
+):
+    me = lax.axis_index("dev")
+    core = lax.rem(me, 2)
+    chip = me // 2
+    x, y = chip // SIDE, lax.rem(chip, SIDE)
+    other = 1 - core
+
+    def device(dx, dy):
+        return (lax.rem(x + dx, SIDE) * SIDE + lax.rem(y + dy, SIDE)) * 2 + core
+
+    def owner(phase, major, minor):
+        dx, dy = (major, minor) if phase == 0 else (minor, major)
+        return lax.rem(x + dx, SIDE) * SIDE + lax.rem(y + dy, SIDE)
+
+    def along_major(phase, step):
+        return device(step, 0) if phase == 0 else device(0, step)
+
+    def along_minor(phase, step):
+        return along_major(1 - phase, step)
+
+    partner = me + 1 - 2 * core
+    barrier = pltpu.get_barrier_semaphore()
+    for peer in (partner, device(1, 0), device(3, 0), device(0, 1), device(0, 3)):
+        pl.semaphore_signal(barrier, inc=1, device_id={"dev": peer}, device_id_type=MESH)
+    pl.semaphore_wait(barrier, 5)
+
+    def remote(src, dst, number, peer):
+        return pltpu.make_async_remote_copy(
+            src_ref=src, dst_ref=dst, send_sem=send_sem.at[number], recv_sem=recv_sem.at[number],
+            device_id={"dev": peer}, device_id_type=MESH,
+        )
+
+    slot_copy = remote(slots_ref.at[other], sl_recv, 16, partner)
+    gw_copy = remote(gw_ref.at[:, other], gw_recv, 17, partner)
+    slot_copy.start()
+    order = [(2, dy) for dy in (0, 1, 2, 3)] + [(dx, 2) for dx in (0, 1, 3)]
+    order += [(dx, dy) for dx in (1, 3, 0) for dy in (1, 3, 0)]
+    pair = {}
+    for number, (dx, dy) in enumerate(order):
+        o = owner(0, dx, dy)
+        pair[dx, dy] = remote(packed_ref.at[other, o], pk_recv.at[o], number, partner)
+        pair[dx, dy].start()
+    gw_copy.start()
+    slot_copy.wait_recv()
+    arrived = set()
+
+    def need(phase, major, minors):
+        for minor in minors:
+            key = (major, minor) if phase == 0 else (minor, major)
+            if key not in arrived:
+                arrived.add(key)
+                pair[key].wait_recv()
+
+    def block(phase, major, minor):
+        o = owner(phase, major, minor)
+        ids = lax.broadcasted_iota(jnp.int32, (HALF, CAP), 0) + phase * HALF
+        mine = jnp.where(slots_ref[core, o] == ids, 1.0, 0.0).astype(bf16)
+        theirs = jnp.where(sl_recv[o] == ids, 1.0, 0.0).astype(bf16)
+        return jnp.dot(mine, packed_ref[core, o], preferred_element_type=f32) + jnp.dot(
+            theirs, pk_recv[o], preferred_element_type=f32
+        )
+
+    def gw_block(phase, major, minor):
+        o = owner(phase, major, minor)
+        at = pl.ds(phase * GW_HALF, GW_HALF)
+        return gw_ref[o, core, at, :] + gw_recv[o, at, :]
+
+    copies = []
+
+    def copy1(phase, j):
+        step = 1 if j < 2 else 3
+        return remote(s1.at[phase, j], r1.at[phase, j], 18 + phase * 4 + j, along_major(phase, step))
+
+    def copy2(phase, way, j):
+        step = 1 if way == 0 else 3
+        return remote(
+            s2.at[phase, way, j], r2.at[phase, way, j], 26 + phase * 8 + way * 4 + j,
+            along_major(phase, step),
+        )
+
+    def small(src, dst, number, peer):
+        c = remote(src, dst, number, peer)
+        copies.append(c)
+        return c
+
+    for phase in range(2):
+        need(phase, 2, range(4))
+        for j in range(4):
+            s1[phase, j] = block(phase, 2, j).astype(bf16)
+            c = copy1(phase, j)
+            c.start()
+            copies.append(c)
+
+    gw_copy.wait_recv()
+    g1 = {}
+    for phase in range(2):
+        for way in range(2):
+            for j in (2 * way, 2 * way + 1):
+                gs1[phase, j] = gw_block(phase, 2, j)
+            at = pl.ds(2 * way, 2)
+            g1[phase, way] = small(
+                gs1.at[phase, at], gr1.at[phase, at], 42 + phase * 2 + way,
+                along_major(phase, 1 + 2 * way),
+            )
+            g1[phase, way].start()
+
+    sent2 = {}
+
+    def second(phase, way, j, add):
+        total = block(phase, 1 + 2 * way, j)
+        if add:
+            copies_by[phase, j].wait_recv()
+            total = total + r1[phase, j].astype(f32)
+        s2[phase, way, j] = total.astype(bf16)
+        sent2[phase, way, j] = copy2(phase, way, j)
+        sent2[phase, way, j].start()
+
+    copies_by = {(phase, j): copies[phase * 4 + j] for phase in range(2) for j in range(4)}
+    for phase in range(2):
+        for way, j in ((0, 2), (1, 1), (0, 3), (1, 0)):
+            need(phase, 1 + 2 * way, (j,))
+            second(phase, way, j, False)
+    for phase in range(2):
+        for way, j in ((1, 2), (0, 1), (1, 3), (0, 0)):
+            need(phase, 1 + 2 * way, (j,))
+            second(phase, way, j, True)
+    g2 = {}
+    for phase in range(2):
+        for way in range(2):
+            g1[phase, way].wait_recv()
+            for j in range(4):
+                total = gw_block(phase, 1 + 2 * way, j)
+                if j // 2 == way:
+                    total = total + gr1[phase, j]
+                gs2[phase, way, j] = total
+            g2[phase, way] = small(
+                gs2.at[phase, way], gr2.at[phase, way], 46 + phase * 2 + way,
+                along_major(phase, 1 + 2 * way),
+            )
+            g2[phase, way].start()
+    for phase in range(2):
+        need(phase, 0, range(4))
+        for j in range(4):
+            own[phase, j] = block(phase, 0, j)
+            gown[phase, j] = gw_block(phase, 0, j)
+
+    def gathered(phase, j):
+        for way in range(2):
+            sent2[phase, way, j].wait_recv()
+        return own[phase, j] + r2[phase, 0, j].astype(f32) + r2[phase, 1, j].astype(f32)
+
+    sent3, sent4, g3, g4 = {}, {}, {}, {}
+    quarter = HALF // 2
+    for phase in range(2):
+        total = gathered(phase, 2)
+        for way in range(2):
+            s3[phase, way] = total[way * quarter : (way + 1) * quarter].astype(bf16)
+            sent3[phase, way] = small(
+                s3.at[phase, way], r3.at[phase, way], 50 + phase * 2 + way,
+                along_minor(phase, 1 + 2 * way),
+            )
+            sent3[phase, way].start()
+    for phase in range(2):
+        for way in range(2):
+            g2[phase, way].wait_recv()
+        for j in range(4):
+            gown[phase, j] = gown[phase, j] + gr2[phase, 0, j] + gr2[phase, 1, j]
+        for way in range(2):
+            gs3[phase, way] = gown[phase, 2, 8 * way : 8 * way + 8]
+            g3[phase, way] = small(
+                gs3.at[phase, way], gr3.at[phase, way], 54 + phase * 2 + way,
+                along_minor(phase, 1 + 2 * way),
+            )
+            g3[phase, way].start()
+    for phase in range(2):
+        for way in range(2):
+            total = gathered(phase, 1 + 2 * way)
+            sent3[phase, way].wait_recv()
+            for part in range(2):
+                at = slice(part * quarter, (part + 1) * quarter)
+                piece = total[at]
+                if part == way:
+                    piece = piece + r3[phase, way].astype(f32)
+                s4[phase, way, at] = piece.astype(bf16)
+            sent4[phase, way] = small(
+                s4.at[phase, way], r4.at[phase, way], 58 + phase * 2 + way,
+                along_minor(phase, 1 + 2 * way),
+            )
+            sent4[phase, way].start()
+            g3[phase, way].wait_recv()
+            for part in range(2):
+                at = slice(8 * part, 8 * part + 8)
+                piece = gown[phase, 1 + 2 * way, at]
+                if part == way:
+                    piece = piece + gr3[phase, way]
+                gs4[phase, way, at] = piece
+            g4[phase, way] = small(
+                gs4.at[phase, way], gr4.at[phase, way], 62 + phase * 2 + way,
+                along_minor(phase, 1 + 2 * way),
+            )
+            g4[phase, way].start()
+    for phase in range(2):
+        own[phase, 0] = gathered(phase, 0)
+    for phase in range(2):
+        for way in range(2):
+            sent4[phase, way].wait_recv()
+            g4[phase, way].wait_recv()
+        out_ref[pl.ds(phase * HALF, HALF), :] = (
+            own[phase, 0] + r4[phase, 0].astype(f32) + r4[phase, 1].astype(f32)
+        )
+        gw_out[pl.ds(phase * GW_HALF, GW_HALF), :] = gown[phase, 0] + gr4[phase, 0] + gr4[phase, 1]
+    for c in [slot_copy, gw_copy, *pair.values(), *copies, *sent2.values()]:
+        c.wait_send()
+
+
+def reduce_rows(packed, slots, grad_weight):
+    vmem = pl.BlockSpec(memory_space=pltpu.VMEM)
+    cols = grad_weight.shape[-1]
+    halves = (HALF, E)
+    small = (GW_HALF, cols)
+    return pl.pallas_call(
+        reduce_kernel,
+        out_shape=(
+            jax.ShapeDtypeStruct((2 * HALF, E), f32),
+            jax.ShapeDtypeStruct((2 * GW_HALF, cols), f32),
+        ),
+        in_specs=[vmem, vmem, vmem],
+        out_specs=(vmem, vmem),
+        scratch_shapes=[
+            pltpu.VMEM((16, CAP, E), bf16),
+            pltpu.VMEM((16, 1, CAP), jnp.int32),
+            pltpu.VMEM((16, 2 * GW_HALF, cols), f32),
+            pltpu.VMEM((2, 4, *halves), bf16),
+            pltpu.VMEM((2, 4, *halves), bf16),
+            pltpu.VMEM((2, 2, 4, *halves), bf16),
+            pltpu.VMEM((2, 2, 4, *halves), bf16),
+            pltpu.VMEM((2, 4, *halves), f32),
+            pltpu.VMEM((2, 2, HALF // 2, E), bf16),
+            pltpu.VMEM((2, 2, HALF // 2, E), bf16),
+            pltpu.VMEM((2, 2, *halves), bf16),
+            pltpu.VMEM((2, 2, *halves), bf16),
+            pltpu.VMEM((2, 4, *small), f32),
+            pltpu.VMEM((2, 4, *small), f32),
+            pltpu.VMEM((2, 2, 4, *small), f32),
+            pltpu.VMEM((2, 2, 4, *small), f32),
+            pltpu.VMEM((2, 4, *small), f32),
+            pltpu.VMEM((2, 2, GW_HALF // 2, cols), f32),
+            pltpu.VMEM((2, 2, GW_HALF // 2, cols), f32),
+            pltpu.VMEM((2, 2, *small), f32),
+            pltpu.VMEM((2, 2, *small), f32),
+            pltpu.SemaphoreType.DMA((66,)),
+            pltpu.SemaphoreType.DMA((66,)),
+        ],
+        compiler_params=pltpu.CompilerParams(collective_id=0, has_side_effects=True),
+        name="reduce_rows",
+    )(packed, slots, grad_weight)
+
+
 def shards(grad_out, pooled, compress_w, owner_ids, slot_ids, touched, table, accum):
     owners = lax.axis_size("dev")
     moved = lax.all_to_all(grad_out, "tower", split_axis=1, concat_axis=0, tiled=True)
@@ -162,9 +413,9 @@
     pooled_rows = pooled[0, 0]
     weight = compress_w[0]
     occurrences = owner_ids.shape[2]
-    touch_count = touched.shape[2]
     slot_total = owners * CAP
-    targets_own = owner_ids[0, 0, :, 0]
+    owner_own = owner_ids[0, 0, :, 0]
+    targets_own = (owner_own % 2) * (owners // 2) + owner_own // 2
     slots_own = slot_ids[0, 0]
     owner_iota = lax.broadcasted_iota(jnp.int32, (owners, occurrences), 0)
     matches = targets_own[None, :] == owner_iota
@@ -181,15 +432,14 @@
     packed_slots = jnp.dot(parts, at_rank, preferred_element_type=f32)
     row_slots = (packed_slots[:owners] * 32 + packed_slots[owners:]).astype(jnp.int32)
 
-    send_values, grad_weight = dense_pack(dest, grad_tower, pooled_rows, weight, slot_total)
-    send_values = send_values.reshape(owners, CAP, E)
-    recv_values, recv_slots = (
-        lax.all_to_all(send_values, "dev", split_axis=0, concat_axis=0, tiled=True),
-        lax.all_to_all(row_slots, "dev", split_axis=0, concat_axis=0, tiled=True),
+    packed, grad_weight = dense_pack(dest, grad_tower, pooled_rows, weight, slot_total)
+    chips = owners // 2
+    row_grad, grad_weight = reduce_rows(
+        packed.reshape(2, chips, CAP, E),
+        row_slots.reshape(2, chips, 1, CAP),
+        grad_weight.reshape(chips, 2, -1, grad_weight.shape[1]),
     )
-    row_grad = accumulate(recv_values.reshape(-1, E), recv_slots.reshape(-1), touch_count)
     new_table, new_accum = update(touched[0, 0], row_grad, table[0], accum[0])
-    grad_weight = lax.psum_scatter(grad_weight, "dev", scatter_dimension=0, tiled=True)
     return (grad_weight[None], new_table[None], new_accum[None])
 
 

time: 154 us -> 86.2 us (0.56)
  waiting for transfers between devices: 64 us -> 0.01 us
  Pallas kernels: 19.8 us -> 63.1 us
  matrix products: 21.9 us -> 3.31 us
  starting transfers between devices: 25.5 us -> 9 us
  between operations: 14.1 us -> 0.7 us
  local copies, waits for them, and re-layouts: 4.06 us -> 6 us
    all_to_all x2 -> x0, waiting for transfers between devices: 50.8 us -> none  [the longest x1 50.8 us: shards(): lax.all_to_all(send_values, 'dev', split_axis=0, concat_axis=0, tiled=True)]
    pallas_call x0 -> x1, Pallas kernels: none -> 42.9 us  [reduce_rows(): pl.pallas_call(reduce_kernel, out_shape=(jax.ShapeDtypeStruct((2 * HALF,...]
    dot_general x4 -> x0, matrix products: 17.8 us -> none  [add_block(): jnp.dot(onehot, block_pair[0], preferred_element_type=jnp.float32)]
    all_to_all x2 -> x0, starting transfers between devices: 16.4 us -> none  [the longest x1 8.85 us: shards(): lax.all_to_all(row_slots, 'dev', split_axis=0, concat_axis=0, tiled=True)]
    reduce_scatter x1 -> x0, waiting for transfers between devices: 13.2 us -> none  [shards(): lax.psum_scatter(grad_weight, 'dev', scatter_dimension=0, tiled=True)]
    unnamed x7 -> x6, local copies, waits for them, and re-layouts: 1.6 us -> 3.6 us
  transfers between devices with their start and end apart: 4 -> 1, of which waited for: 2 -> 0; matrix products, arithmetic and copies ran while one was open for 18% -> 11% of each run, Pallas kernels for 13% -> 0%
where the time goes in v2:
time: 86.2 us; the launch traced here: 85.7 us
  Pallas kernels  63.1 us (73%)
  starting transfers between devices  9 us (10%)
  local copies, waits for them, and re-layouts  6 us (7%)
  other arithmetic  3.53 us (4%)
  matrix products  3.31 us (4%)
    pallas_call x1, Pallas kernels, reduce_rows(): pl.pallas_call(reduce_kernel, out_shape=(jax.ShapeDtypeStruct((2 * HALF,...  42.9 us
    pallas_call x1, Pallas kernels, dense_pack(): pl.pallas_call(dense_pack_kernel, out_shape=(jax.ShapeDtypeStruct((slot_t...  13.8 us
    all_to_all x1, starting transfers between devices, shards(): lax.all_to_all(grad_out, 'tower', split_axis=1, concat_axis=0, tiled=True)  9 us
    pallas_call x1, Pallas kernels, update(): pl.pallas_call(update_kernel, out_shape=(jax.ShapeDtypeStruct(table.shape...  6.47 us
    unnamed x6, local copies, waits for them, and re-layouts  3.6 us
    dot_general x1, matrix products, shards(): packed_slots = jnp.dot(parts, at_rank, preferred_element_type=f32)  2.88 us
  transfers between devices with their start and end apart: 1, of which 0 were waited for; matrix products, arithmetic and copies ran while one was open for 11% of the time, Pallas kernels for 0%

profile of v2, /device:TPU:1, one launch (start us, length us, event | category | flops | bytes accessed | tf_op | source)
XLA Modules:
  0.0 85.7 jit_solution(4373612268078327041)
XLA Ops:
  0.6 1.6 %copy.14 = bf16[32,8,256]{2,0,1:T(8,128)(2,1)} copy(bf16[32,8,256]{2,1,0:T(8,128)(2,1)} %param.8) | data formatting | bytes 262144 | tf_op args[0]
  2.2 9.0 %all-to-all-start = ((bf16[32,8,256]{2,0,1:T(8,128)(2,1)}), bf16[32,8,256]{2,0,1:T(8,128)(2,1)S(1)}, u32[]{:S(2)}, u32[]{:S(2)}) async-start(bf16[32,8,256]{2,0,1:T(8,128)(2,1)} %copy.14), calls=%async_computation | async-start | bytes 262144 | tf_op jit(solution)/shard_map/all_to_all | solution.py:411
  11.2 0.8 fusion.13
  12.0 0.3 fusion.5
  12.3 0.6 slice_reduce_fusion
  13.0 0.1 fusion.22
  13.1 0.4 select_reduce_fusion
  13.5 0.8 add_select_fusion.1
  14.3 1.4 %multiply_add_fusion = (s32[8192]{0:T(1024)}, s32[8192]{0:T(1024)S(1)}) fusion(s32[64,128]{1,0:T(8,128)S(1)} %select_reduce_fusion, s32[8192]{0:T(1024)} %bitcast.33), kind=kLoop, calls=%fused_computation.43 | loop fusion | flops 188416 | bytes 131072 | tf_op jit(solution)/shard_map/add | solution.py:424
  15.7 0.2 select_convert_fusion.1
  15.8 0.0 copy-start.1
  15.8 2.9 %fusion = f32[64,512]{1,0:T(8,128)S(1)} fusion(s32[8192]{0:T(1024)S(1)} %bitcast.31, bf16[32,8192]{1,0:T(8,128)(2,1)S(1)} %get-tuple-element.18, bf16[32,8192]{1,0:T(8,128)(2,1)S(1)} %get-tuple-element.17), kind=kOutput, calls=%fused_computation.1 | convolution fusion | flops 543162368 | bytes 1212416 | tf_op jit(solution)/shard_map/dot_general | solution.py:432
  18.7 0.7 reshape.179.slots_ref
  19.5 0.0 copy-done.1
  19.5 1.1 %copy.15.col_ref = s32[1024,1]{1,0:T(8,128)} copy(s32[1024,1]{0,1:T(1,128)S(1)} %bitcast.38) | data formatting | bytes 8192 | tf_op jit(solution)/shard_map/broadcast_in_dim;squeeze | solution.py:138
  20.5 0.0 all-to-all-done
  20.5 0.0 copy-start
  20.5 0.6 copy-done
  21.2 13.8 %dense_pack.1 = (bf16[16384,128]{1,0:T(8,128)(2,1)}, f32[1024,256]{1,0:T(8,128)}) custom-call(s32[8192]{0:T(1024)} %get-tuple-element.15.dest_ref, bf16[256,256]{1,0:T(8,128)(2,1)} %bitcast.30, bf16[256,1024]{1,0:T(8,128)(2,1)} %bitcast.28, bf16[1024,256]{1,0:T(8,128)(2,1)} %bitcast.29), custom_call_target="tpu_custom_call" | custom-call | tf_op jit(solution)/shard_map/dense_pack/pallas_call | solution.py:85
  34.9 42.9 %reduce_rows.1 = (f32[1024,128]{1,0:T(8,128)}, f32[32,256]{1,0:T(8,128)}) custom-call(bf16[2,16,512,128]{3,2,1,0:T(8,128)(2,1)} %bitcast.25, s32[2,16,1,512]{3,2,1,0:T(1,128)} %reshape.179.slots_ref, f32[16,2,32,256]{3,2,1,0:T(8,128)} %bitcast.27), custom_call_target="tpu_custom_call" | custom-call | tf_op jit(solution)/shard_map/reduce_rows/pallas_call | solution.py:371
  77.8 6.5 %row_update.1 = (f32[4096,128]{1,0:T(8,128)}, f32[32,128]{1,0:T(8,128)}) custom-call(s32[1024]{0:T(1024)} %bitcast.37, s32[1024,1]{1,0:T(8,128)} %copy.15.col_ref, f32[1024,128]{1,0:T(8,128)} %get-tuple-element.12.grad_ref, f32[4096,128]{1,0:T(8,128)} %bitcast.26, f32[32,128]{1,0:T(8,128)} %bitcast.36), custom_call_target="tpu_custom_call" | custom-call | tf_op jit(solution)/shard_map/row_update/pallas_call | solution.py:128
  84.3 1.4 %copy.17 = f32[1,32,256]{2,1,0:T(8,128)} copy(f32[1,32,256]{2,1,0:T(8,128)} %bitcast.35) | data formatting | bytes 65536
  (1 shorter events, 0.0 us)
Async XLA Ops:
  2.2 18.3 %all-to-all-start = ((bf16[32,8,256]{2,0,1:T(8,128)(2,1)}), bf16[32,8,256]{2,0,1:T(8,128)(2,1)S(1)}, u32[]{:S(2)}, u32[]{:S(2)}) async-start(bf16[32,8,256]{2,0,1:T(8,128)(2,1)} %copy.14), calls=%async_computation | async-start | bytes 262144 | tf_op jit(solution)/shard_map/all_to_all | solution.py:411
  15.8 3.6 %copy-start.1 = (s32[1,1,1024]{2,1,0:T(1,128)S(1)}, s32[1,1,1024]{2,1,0:T(1,128)}, u32[]{:S(2)}) copy-start(s32[1,1,1024]{2,1,0:T(1,128)} %param.13) | copy-start | bytes 12292
  20.5 0.6 copy-start

commit v3 on v2

--- a/solution.py
+++ b/solution.py
@@ -1,5 +1,3 @@
-import math
-
 import jax
 import jax.numpy as jnp
 from jax import lax
@@ -10,6 +8,8 @@
 E = 128
 HOT = 4
 CAP = 512
+FEATS = 8
+OWNERS = 32
 
 
 learn_rate = 0.1
@@ -20,25 +20,134 @@
 bf16 = jnp.bfloat16
 
 
-def count_before(matches):
-    row_total, length = matches.shape
-    width = math.gcd(length, 128)
-    blocks = length // width
-    marks = matches.astype(jnp.bfloat16).reshape(row_total, blocks, width)
-    lower = lax.broadcasted_iota(jnp.int32, (width, width), 0)
-    upper = lax.broadcasted_iota(jnp.int32, (width, width), 1)
-    inclusive = (lower <= upper).astype(jnp.bfloat16)
-    within = jnp.einsum("rbi,ij->rbj", marks, inclusive, preferred_element_type=jnp.float32)
-    totals = within[:, :, width - 1]
-    block_a = lax.broadcasted_iota(jnp.int32, (blocks, blocks), 0)
-    block_b = lax.broadcasted_iota(jnp.int32, (blocks, blocks), 1)
-    strict = (block_a < block_b).astype(jnp.float32)
-    offsets = jnp.dot(totals, strict, precision=highest, preferred_element_type=jnp.float32)
-    ranks = within + offsets[:, :, None]
-    return ranks.reshape(row_total, length).astype(jnp.int32) - 1
-
-
-def dense_pack_kernel(dest_ref, grad_ref, pooled_ref, w_ref, packed_ref, gw_ref, bag_ref, rows_ref):
+def front_kernel(
+    grad_ref, pooled_ref, w_ref, owner_ref, slot_ref, bags_ref, gw_ref, dest_ref, slots_ref,
+    sbuf, rbuf, marks_ref, count_ref, rank_ref, list_ref, send_sem, recv_sem,
+):
+    me = lax.axis_index("tower")
+    towers = grad_ref.shape[1]
+    barrier = pltpu.get_barrier_semaphore()
+    for k in range(1, towers):
+        pl.semaphore_signal(
+            barrier, inc=1, device_id={"tower": lax.rem(me + k, towers)}, device_id_type=MESH
+        )
+    sent = grad_ref[...].astype(f32)
+    for t in range(towers):
+        sbuf[t] = sent[:, t, :].astype(bf16)
+    pl.semaphore_wait(barrier, towers - 1)
+    copies = []
+    for k in sorted(range(1, towers), key=lambda k: -min(k, towers - k)):
+        peer = lax.rem(me + k, towers)
+        c = pltpu.make_async_remote_copy(
+            src_ref=sbuf.at[peer], dst_ref=rbuf.at[me], send_sem=send_sem.at[k],
+            recv_sem=recv_sem.at[k], device_id={"tower": peer}, device_id_type=MESH,
+        )
+        c.start()
+        copies.append(c)
+    rbuf[me] = sbuf[me]
+
+    blocks = owner_ref.shape[0]
+    sub = lax.broadcasted_iota(jnp.int32, (OWNERS, E), 0)
+    owner = owner_ref[...]
+    target = (owner & 1) * (OWNERS // 2) + (owner >> 1)
+    for b in range(blocks):
+        marks_ref[b * OWNERS : (b + 1) * OWNERS, :] = jnp.where(
+            target[b : b + 1, :] == sub, 1.0, 0.0
+        ).astype(bf16)
+    row = lax.broadcasted_iota(jnp.int32, (E, 2 * E), 0)
+    col = lax.broadcasted_iota(jnp.int32, (E, 2 * E), 1)
+    before = jnp.where(row <= col, 1.0, 0.0).astype(bf16)
+    count_ref[...] = jnp.dot(marks_ref[...], before, preferred_element_type=f32)
+    run = jnp.zeros((OWNERS, E), f32)
+    for b in range(blocks):
+        at = slice(b * OWNERS, (b + 1) * OWNERS)
+        mark = marks_ref[at, :].astype(f32)
+        rank = jnp.sum(mark * (count_ref[at, :E] + run), axis=0, keepdims=True)
+        rank_ref[b : b + 1, :] = rank.astype(jnp.int32) - 1
+        run = run + count_ref[at, E:]
+    dest_ref[...] = target * CAP + rank_ref[...]
+
+    list_ref[...] = jnp.zeros(list_ref.shape, f32)
+    step = 8
+
+    @pl.loop(0, blocks // step)
+    def _(c):
+        at = pl.ds(pl.multiple_of(c * step, step), step)
+        ranks = rank_ref[at, :]
+        slots = slot_ref[at, :]
+        high = (slots >> 5).astype(f32)
+        low = (slots & 31).astype(f32)
+        ids = lax.broadcasted_iota(jnp.int32, (CAP, E), 0)
+        at_rank, parts = [], []
+        for j in range(step):
+            one = slice(j, j + 1)
+            at_rank.append(jnp.where(ranks[one] == ids, 1.0, 0.0).astype(bf16))
+            base = pl.multiple_of(c * (step * OWNERS) + j * OWNERS, OWNERS)
+            mark = marks_ref[pl.ds(base, OWNERS), :].astype(f32)
+            parts.append(
+                jnp.concatenate([mark * high[one], mark * low[one]], axis=0).astype(bf16)
+            )
+        list_ref[...] += lax.dot_general(
+            jnp.concatenate(parts, axis=1), jnp.concatenate(at_rank, axis=1),
+            (((1,), (1,)), ((), ())), preferred_element_type=f32,
+        )
+
+    slots_ref[...] = (list_ref[:OWNERS] * 32.0 + list_ref[OWNERS:]).astype(jnp.int32)
+
+    preact = jnp.dot(pooled_ref[...], w_ref[...], preferred_element_type=f32)
+    sigma = 1.0 / (1.0 + jnp.exp(-preact))
+    for c in copies:
+        c.wait_recv()
+    moved = rbuf[...].reshape(preact.shape)
+    grad_pre = (moved.astype(f32) * sigma * (1.0 + preact * (1.0 - sigma))).astype(bf16)
+    gw_ref[...] = lax.dot_general(
+        pooled_ref[...], grad_pre, (((0,), (0,)), ((), ())), preferred_element_type=f32
+    )
+    group = preact.shape[0]
+    for f in range(w_ref.shape[0] // E):
+        bags_ref[f * group : (f + 1) * group, :] = (
+            lax.dot_general(
+                grad_pre, w_ref[f * E : (f + 1) * E, :], (((1,), (1,)), ((), ())),
+                preferred_element_type=f32,
+            )
+            .astype(bf16)
+            .astype(f32)
+        )
+    for c in copies:
+        c.wait_send()
+
+
+def front(grad_out, pooled_rows, weight, owner_rows, slot_rows):
+    vmem = pl.BlockSpec(memory_space=pltpu.VMEM)
+    samples, towers, cols = grad_out.shape
+    group, depth = pooled_rows.shape
+    blocks = owner_rows.shape[0]
+    return pl.pallas_call(
+        front_kernel,
+        out_shape=(
+            jax.ShapeDtypeStruct((depth // E * group, E), f32),
+            jax.ShapeDtypeStruct(weight.shape, f32),
+            jax.ShapeDtypeStruct(owner_rows.shape, jnp.int32),
+            jax.ShapeDtypeStruct((OWNERS, CAP), jnp.int32),
+        ),
+        in_specs=[vmem] * 5,
+        out_specs=(vmem,) * 4,
+        scratch_shapes=[
+            pltpu.VMEM((towers, samples, cols), bf16),
+            pltpu.VMEM((towers, samples, cols), bf16),
+            pltpu.VMEM((blocks * OWNERS, E), bf16),
+            pltpu.VMEM((blocks * OWNERS, 2 * E), f32),
+            pltpu.VMEM((blocks, E), jnp.int32),
+            pltpu.VMEM((2 * OWNERS, CAP), f32),
+            pltpu.SemaphoreType.DMA((towers,)),
+            pltpu.SemaphoreType.DMA((towers,)),
+        ],
+        compiler_params=pltpu.CompilerParams(collective_id=1, has_side_effects=True),
+        name="front",
+    )(grad_out, pooled_rows, weight, owner_rows, slot_rows)
+
+
+def pack_kernel(dest_ref, bag_ref, packed_ref, rows_ref):
     total = rows_ref.shape[0]
     step = 512
 
@@ -46,32 +155,16 @@
     def _(i):
         rows_ref[pl.ds(pl.multiple_of(i * step, step), step), :] = jnp.zeros((step, E), f32)
 
-    preact = jnp.dot(pooled_ref[...], w_ref[...], preferred_element_type=f32)
-    sigma = 1.0 / (1.0 + jnp.exp(-preact))
-    grad_pre = (grad_ref[...].astype(f32) * sigma * (1.0 + preact * (1.0 - sigma))).astype(bf16)
-    gw_ref[...] = lax.dot_general(
-        pooled_ref[...], grad_pre, (((0,), (0,)), ((), ())), preferred_element_type=f32
-    )
-    feats, group, _ = bag_ref.shape
-    for f in range(feats):
-        bag_ref[f] = (
-            lax.dot_general(
-                grad_pre,
-                w_ref[f * E : (f + 1) * E, :],
-                (((1,), (1,)), ((), ())),
-                preferred_element_type=f32,
-            )
-            .astype(bf16)
-            .astype(f32)
-        )
-
-    @pl.loop(0, group)
-    def _(g):
-        for f in range(feats):
-            row = bag_ref[f, pl.ds(g, 1), :]
-            for k in range(HOT):
-                d = dest_ref[g * (feats * HOT) + f * HOT + k]
-                rows_ref[pl.ds(d, 1), :] = row
+    group = bag_ref.shape[0] // FEATS
+
+    @pl.loop(0, group // 2)
+    def _(i):
+        for g in (2 * i, 2 * i + 1):
+            for f in range(FEATS):
+                row = bag_ref[pl.ds(f * group + g, 1), :]
+                for k in range(HOT):
+                    d = dest_ref[g * (FEATS * HOT) + f * HOT + k]
+                    rows_ref[pl.ds(d, 1), :] = row
 
     @pl.loop(0, total // step)
     def _(i):
@@ -79,34 +172,35 @@
         packed_ref[at, :] = rows_ref[at, :].astype(bf16)
 
 
-def dense_pack(dest, grad_tower, pooled_rows, weight, slot_total):
+def pack(dest, bags, slot_total):
     vmem = pl.BlockSpec(memory_space=pltpu.VMEM)
-    group, depth = pooled_rows.shape
     return pl.pallas_call(
-        dense_pack_kernel,
-        out_shape=(
-            jax.ShapeDtypeStruct((slot_total, E), bf16),
-            jax.ShapeDtypeStruct(weight.shape, f32),
-        ),
-        in_specs=[pl.BlockSpec(memory_space=pltpu.SMEM), vmem, vmem, vmem],
-        out_specs=(vmem, vmem),
-        scratch_shapes=[
-            pltpu.VMEM((depth // E, group, E), f32),
-            pltpu.VMEM((slot_total, E), f32),
-        ],
-        name="dense_pack",
-    )(dest, grad_tower, pooled_rows, weight)
-
-
-def update_kernel(rows_ref, col_ref, grad_ref, table_ref, accum_ref, out_ref, accum_out, upd_ref):
+        pack_kernel,
+        out_shape=jax.ShapeDtypeStruct((slot_total, E), bf16),
+        in_specs=[pl.BlockSpec(memory_space=pltpu.SMEM), vmem],
+        out_specs=vmem,
+        scratch_shapes=[pltpu.VMEM((slot_total, E), f32)],
+        name="pack",
+    )(dest, bags)
+
+
+def update_kernel(
+    rows_ref, lane_ref, grad_ref, table_ref, accum_ref, gw_ref, out_ref, accum_out, gw_out, upd_ref
+):
+    gw_out[...] = gw_ref[...]
     row_grad = grad_ref[...]
     count = row_grad.shape[0]
     sq_mean = jnp.mean(row_grad * row_grad, axis=1, keepdims=True)
-    col = col_ref[...]
+    col = jnp.concatenate(
+        [
+            jnp.broadcast_to(lane_ref[b : b + 1, :].astype(f32), (E, E)).T
+            for b in range(count // E)
+        ]
+    ).astype(jnp.int32)
     lanes = lax.broadcasted_iota(jnp.int32, (count, E), 1)
     blocks = accum_ref.shape[0]
-    high = (lax.broadcasted_iota(jnp.int32, (count, blocks), 1) == col // E).astype(f32)
-    low = (lanes == lax.rem(col, E)).astype(f32)
+    high = ((col >> 7) == lanes).astype(f32)[:, :blocks]
+    low = ((col & 127) == lanes).astype(f32)
     spread = jnp.dot(high, accum_ref[...], precision=highest, preferred_element_type=f32)
     accum_touched = jnp.sum(spread * low, axis=1, keepdims=True) + sq_mean
     accum_out[...] = accum_ref[...] + lax.dot_general(
@@ -115,28 +209,29 @@
     upd_ref[...] = learn_rate * row_grad / jnp.sqrt(accum_touched + epsilon)
     out_ref[...] = table_ref[...]
 
-    @pl.loop(0, count // 8)
+    @pl.loop(0, count // 16)
     def _(i):
-        for k in range(8):
-            u = i * 8 + k
+        for k in range(16):
+            u = i * 16 + k
             r = rows_ref[u]
             out_ref[pl.ds(r, 1), :] = table_ref[pl.ds(r, 1), :] - upd_ref[pl.ds(u, 1), :]
 
 
-def update(touched, row_grad, table, accum):
+def update(touched, row_grad, table, accum, grad_weight):
     vmem = pl.BlockSpec(memory_space=pltpu.VMEM)
-    new_table, new_accum = pl.pallas_call(
+    new_table, new_accum, grad_weight = pl.pallas_call(
         update_kernel,
         out_shape=(
             jax.ShapeDtypeStruct(table.shape, f32),
             jax.ShapeDtypeStruct((accum.shape[0] // E, E), f32),
+            jax.ShapeDtypeStruct(grad_weight.shape, f32),
         ),
-        in_specs=[pl.BlockSpec(memory_space=pltpu.SMEM), vmem, vmem, vmem, vmem],
-        out_specs=(vmem, vmem),
+        in_specs=[pl.BlockSpec(memory_space=pltpu.SMEM), vmem, vmem, vmem, vmem, vmem],
+        out_specs=(vmem, vmem, vmem),
         scratch_shapes=[pltpu.VMEM(row_grad.shape, f32)],
         name="row_update",
-    )(touched, touched[:, None], row_grad, table, accum.reshape(-1, E))
-    return new_table, new_accum.reshape(-1)
+    )(touched, touched.reshape(-1, E), row_grad, table, accum.reshape(-1, E), grad_weight)
+    return new_table, new_accum.reshape(-1), grad_weight
 
 
 SIDE = 4
@@ -407,39 +502,23 @@
 
 
 def shards(grad_out, pooled, compress_w, owner_ids, slot_ids, touched, table, accum):
-    owners = lax.axis_size("dev")
-    moved = lax.all_to_all(grad_out, "tower", split_axis=1, concat_axis=0, tiled=True)
-    grad_tower = moved[:, 0, :]
-    pooled_rows = pooled[0, 0]
-    weight = compress_w[0]
-    occurrences = owner_ids.shape[2]
-    slot_total = owners * CAP
-    owner_own = owner_ids[0, 0, :, 0]
-    targets_own = (owner_own % 2) * (owners // 2) + owner_own // 2
-    slots_own = slot_ids[0, 0]
-    owner_iota = lax.broadcasted_iota(jnp.int32, (owners, occurrences), 0)
-    matches = targets_own[None, :] == owner_iota
-    ranks = count_before(matches)
-    own_rank = jnp.sum(jnp.where(matches, ranks, 0), axis=0)
-    dest = targets_own * CAP + own_rank
-    parts = jnp.concatenate(
-        [
-            jnp.where(matches, slots_own[None, :] // 32, 0).astype(bf16),
-            jnp.where(matches, slots_own[None, :] % 32, 0).astype(bf16),
-        ]
+    chips = OWNERS // 2
+    bags, grad_weight, dest, slots = front(
+        grad_out,
+        pooled[0, 0],
+        compress_w[0],
+        owner_ids.reshape(-1, E),
+        slot_ids.reshape(-1, E),
     )
-    at_rank = (own_rank[:, None] == lax.broadcasted_iota(jnp.int32, (occurrences, CAP), 1)).astype(bf16)
-    packed_slots = jnp.dot(parts, at_rank, preferred_element_type=f32)
-    row_slots = (packed_slots[:owners] * 32 + packed_slots[owners:]).astype(jnp.int32)
-
-    packed, grad_weight = dense_pack(dest, grad_tower, pooled_rows, weight, slot_total)
-    chips = owners // 2
+    packed = pack(dest.reshape(-1), bags, OWNERS * CAP)
     row_grad, grad_weight = reduce_rows(
         packed.reshape(2, chips, CAP, E),
-        row_slots.reshape(2, chips, 1, CAP),
+        slots.reshape(2, chips, 1, CAP),
         grad_weight.reshape(chips, 2, -1, grad_weight.shape[1]),
     )
-    new_table, new_accum = update(touched[0, 0], row_grad, table[0], accum[0])
+    new_table, new_accum, grad_weight = update(
+        touched[0, 0], row_grad, table[0], accum[0], grad_weight
+    )
     return (grad_weight[None], new_table[None], new_accum[None])
 
 

time: 86.2 us -> 78.6 us (0.912)
  Pallas kernels: 63.1 us -> 76.2 us
  starting transfers between devices: 9 us -> 0 us
  local copies, waits for them, and re-layouts: 6 us -> 1.54 us
  other arithmetic: 3.53 us -> 0 us
  matrix products: 3.31 us -> 0 us
    pallas_call x1 -> x2, Pallas kernels: 13.8 us -> 27.4 us  [the longest x1 16 us: front(): pl.pallas_call(front_kernel, out_shape=(jax.ShapeDtypeStruct((depth // E...]
    all_to_all x1 -> x0, starting transfers between devices: 9 us -> none  [shards(): lax.all_to_all(grad_out, 'tower', split_axis=1, concat_axis=0, tiled=True)]
    unnamed x6 -> x0, local copies, waits for them, and re-layouts: 3.6 us -> none
    dot_general x3 -> x0, matrix products: 3.31 us -> none  [the longest x1 2.88 us: shards(): packed_slots = jnp.dot(parts, at_rank, preferred_element_type=f32)]
    add x2 -> x0, other arithmetic: 2.2 us -> none  [the longest x1 1.41 us: shards(): dest = targets_own * CAP + own_rank]
    another operation x1 -> x0, local copies, waits for them, and re-layouts: 1.05 us -> none  [update(): touched[:, None]]
  transfers between devices with their start and end apart: 1 -> 0, of which waited for: 0 -> 0; matrix products, arithmetic and copies ran while one was open for 11% -> 0% of each run, Pallas kernels for 0% -> 0%
where the time goes in v3:
time: 78.6 us; the launch traced here: 78.4 us
  Pallas kernels  76.2 us (97%)
  local copies, waits for them, and re-layouts  1.54 us (2%)
    pallas_call x1, Pallas kernels, reduce_rows(): pl.pallas_call(reduce_kernel, out_shape=(jax.ShapeDtypeStruct((2 * HALF,...  43.1 us
    pallas_call x1, Pallas kernels, front(): pl.pallas_call(front_kernel, out_shape=(jax.ShapeDtypeStruct((depth // E...  16 us
    pallas_call x1, Pallas kernels, pack(): pl.pallas_call(pack_kernel, out_shape=jax.ShapeDtypeStruct((slot_total, E...  11.4 us
    pallas_call x1, Pallas kernels, update(): pl.pallas_call(update_kernel, out_shape=(jax.ShapeDtypeStruct(table.shape...  5.64 us

profile of v3, /device:TPU:1, one launch (start us, length us, event | category | flops | bytes accessed | tf_op | source)
XLA Modules:
  0.0 78.4 jit_solution(9126342172190659219)
XLA Ops:
  0.6 16.0 %front.1 = (f32[2048,128]{1,0:T(8,128)}, f32[1024,256]{1,0:T(8,128)}, s32[64,128]{1,0:T(8,128)}, s32[32,512]{1,0:T(8,128)}) custom-call(bf16[32,8,256]{2,1,0:T(8,128)(2,1)} %grad_ref.1, bf16[256,1024]{1,0:T(8,128)(2,1)} %bitcast.17, bf16[1024,256]{1,0:T(8,128)(2,1)} %bitcast.18, s32[64,128]{1,0:T(8,128)} %bitcast.20, s32[64,128]{1,0:T(8,128)} %bitcast.21), custom_call_target="tpu_custom_call" | custom-call | tf_op jit(solution)/shard_map/front/pallas_call | solution.py:125
  16.6 1.5 %reshape.28.slots_ref = s32[2,16,1,512]{3,2,1,0:T(1,128)} reshape(s32[32,512]{1,0:T(8,128)} %get-tuple-element.14) | data formatting | bytes 131072 | tf_op jit(solution)/shard_map/reshape | solution.py:516
  18.2 11.4 %pack.1 = bf16[16384,128]{1,0:T(8,128)(2,1)} custom-call(s32[8192]{0:T(1024)} %bitcast.19, f32[2048,128]{1,0:T(8,128)} %get-tuple-element.13.bag_ref), custom_call_target="tpu_custom_call" | custom-call | tf_op jit(solution)/shard_map/pack/pallas_call | solution.py:177
  29.6 43.1 %reduce_rows.1 = (f32[1024,128]{1,0:T(8,128)}, f32[32,256]{1,0:T(8,128)}) custom-call(bf16[2,16,512,128]{3,2,1,0:T(8,128)(2,1)} %bitcast.14, s32[2,16,1,512]{3,2,1,0:T(1,128)} %reshape.28.slots_ref, f32[16,2,32,256]{3,2,1,0:T(8,128)} %bitcast.16), custom_call_target="tpu_custom_call" | custom-call | tf_op jit(solution)/shard_map/reduce_rows/pallas_call | solution.py:466
  72.8 5.6 %row_update.1 = (f32[4096,128]{1,0:T(8,128)}, f32[32,128]{1,0:T(8,128)}, f32[32,256]{1,0:T(8,128)}) custom-call(s32[1024]{0:T(1024)} %bitcast.23, s32[8,128]{1,0:T(8,128)} %bitcast.24, f32[1024,128]{1,0:T(8,128)} %get-tuple-element.16.grad_ref, f32[4096,128]{1,0:T(8,128)} %bitcast.15, f32[32,128]{1,0:T(8,128)} %bitcast.22, f32[32,256]{1,0:T(8,128)} %get-tuple-element.17.gw_ref), custom_call_target="tpu_custom_call" | custom-call | tf_op jit(solution)/shard_map/row_update/pallas_call | solution.py:222

commit v4 on v3

--- a/solution.py
+++ b/solution.py
@@ -21,7 +21,7 @@
 
 
 def front_kernel(
-    grad_ref, pooled_ref, w_ref, owner_ref, slot_ref, bags_ref, gw_ref, dest_ref, slots_ref,
+    grad_ref, pooled_ref, w_ref, owner_ref, slot_ref, bags_ref, gw_ref, from_ref, slots_ref,
     sbuf, rbuf, marks_ref, count_ref, rank_ref, list_ref, send_sem, recv_sem,
 ):
     me = lax.axis_index("tower")
@@ -65,10 +65,11 @@
         rank = jnp.sum(mark * (count_ref[at, :E] + run), axis=0, keepdims=True)
         rank_ref[b : b + 1, :] = rank.astype(jnp.int32) - 1
         run = run + count_ref[at, E:]
-    dest_ref[...] = target * CAP + rank_ref[...]
 
     list_ref[...] = jnp.zeros(list_ref.shape, f32)
     step = 8
+    lane = lax.broadcasted_iota(jnp.int32, (OWNERS, E), 1)
+    inner = (((lane >> 2) & 7) * 4 + (lane >> 5)).astype(f32)
 
     @pl.loop(0, blocks // step)
     def _(c):
@@ -84,15 +85,27 @@
             at_rank.append(jnp.where(ranks[one] == ids, 1.0, 0.0).astype(bf16))
             base = pl.multiple_of(c * (step * OWNERS) + j * OWNERS, OWNERS)
             mark = marks_ref[pl.ds(base, OWNERS), :].astype(f32)
+            place = (c * step + j + 1).astype(f32)
             parts.append(
-                jnp.concatenate([mark * high[one], mark * low[one]], axis=0).astype(bf16)
+                jnp.concatenate(
+                    [mark * high[one], mark * low[one], mark * place, mark * inner], axis=0
+                ).astype(bf16)
             )
         list_ref[...] += lax.dot_general(
             jnp.concatenate(parts, axis=1), jnp.concatenate(at_rank, axis=1),
             (((1,), (1,)), ((), ())), preferred_element_type=f32,
         )
 
-    slots_ref[...] = (list_ref[:OWNERS] * 32.0 + list_ref[OWNERS:]).astype(jnp.int32)
+    slots = (list_ref[:OWNERS] * 32.0 + list_ref[OWNERS : 2 * OWNERS]).astype(jnp.int32)
+    for o in range(OWNERS):
+        slots_ref[o] = slots[o : o + 1]
+    group = pooled_ref.shape[0]
+    place = list_ref[2 * OWNERS : 3 * OWNERS].astype(jnp.int32)
+    inner = list_ref[3 * OWNERS :].astype(jnp.int32)
+    source = (inner >> 2) * group + (place - 1) * 4 + (inner & 3)
+    source = jnp.where(place > 0, source, FEATS * group)
+    for q in range(CAP // E):
+        from_ref[q * OWNERS : (q + 1) * OWNERS, :] = source[:, q * E : (q + 1) * E]
 
     preact = jnp.dot(pooled_ref[...], w_ref[...], preferred_element_type=f32)
     sigma = 1.0 / (1.0 + jnp.exp(-preact))
@@ -103,8 +116,8 @@
     gw_ref[...] = lax.dot_general(
         pooled_ref[...], grad_pre, (((0,), (0,)), ((), ())), preferred_element_type=f32
     )
-    group = preact.shape[0]
-    for f in range(w_ref.shape[0] // E):
+    bags_ref[FEATS * group :, :] = jnp.zeros((8, E), f32)
+    for f in range(FEATS):
         bags_ref[f * group : (f + 1) * group, :] = (
             lax.dot_general(
                 grad_pre, w_ref[f * E : (f + 1) * E, :], (((1,), (1,)), ((), ())),
@@ -120,15 +133,15 @@
 def front(grad_out, pooled_rows, weight, owner_rows, slot_rows):
     vmem = pl.BlockSpec(memory_space=pltpu.VMEM)
     samples, towers, cols = grad_out.shape
-    group, depth = pooled_rows.shape
+    group = pooled_rows.shape[0]
     blocks = owner_rows.shape[0]
     return pl.pallas_call(
         front_kernel,
         out_shape=(
-            jax.ShapeDtypeStruct((depth // E * group, E), f32),
+            jax.ShapeDtypeStruct((FEATS * group + 8, E), f32),
             jax.ShapeDtypeStruct(weight.shape, f32),
-            jax.ShapeDtypeStruct(owner_rows.shape, jnp.int32),
-            jax.ShapeDtypeStruct((OWNERS, CAP), jnp.int32),
+            jax.ShapeDtypeStruct((OWNERS * CAP // E, E), jnp.int32),
+            jax.ShapeDtypeStruct((OWNERS, 1, CAP), jnp.int32),
         ),
         in_specs=[vmem] * 5,
         out_specs=(vmem,) * 4,
@@ -138,50 +151,13 @@
             pltpu.VMEM((blocks * OWNERS, E), bf16),
             pltpu.VMEM((blocks * OWNERS, 2 * E), f32),
             pltpu.VMEM((blocks, E), jnp.int32),
-            pltpu.VMEM((2 * OWNERS, CAP), f32),
+            pltpu.VMEM((4 * OWNERS, CAP), f32),
             pltpu.SemaphoreType.DMA((towers,)),
             pltpu.SemaphoreType.DMA((towers,)),
         ],
         compiler_params=pltpu.CompilerParams(collective_id=1, has_side_effects=True),
         name="front",
     )(grad_out, pooled_rows, weight, owner_rows, slot_rows)
-
-
-def pack_kernel(dest_ref, bag_ref, packed_ref, rows_ref):
-    total = rows_ref.shape[0]
-    step = 512
-
-    @pl.loop(0, total // step)
-    def _(i):
-        rows_ref[pl.ds(pl.multiple_of(i * step, step), step), :] = jnp.zeros((step, E), f32)
-
-    group = bag_ref.shape[0] // FEATS
-
-    @pl.loop(0, group // 2)
-    def _(i):
-        for g in (2 * i, 2 * i + 1):
-            for f in range(FEATS):
-                row = bag_ref[pl.ds(f * group + g, 1), :]
-                for k in range(HOT):
-                    d = dest_ref[g * (FEATS * HOT) + f * HOT + k]
-                    rows_ref[pl.ds(d, 1), :] = row
-
-    @pl.loop(0, total // step)
-    def _(i):
-        at = pl.ds(pl.multiple_of(i * step, step), step)
-        packed_ref[at, :] = rows_ref[at, :].astype(bf16)
-
-
-def pack(dest, bags, slot_total):
-    vmem = pl.BlockSpec(memory_space=pltpu.VMEM)
-    return pl.pallas_call(
-        pack_kernel,
-        out_shape=jax.ShapeDtypeStruct((slot_total, E), bf16),
-        in_specs=[pl.BlockSpec(memory_space=pltpu.SMEM), vmem],
-        out_specs=vmem,
-        scratch_shapes=[pltpu.VMEM((slot_total, E), f32)],
-        name="pack",
-    )(dest, bags)
 
 
 def update_kernel(
@@ -240,7 +216,7 @@
 
 
 def reduce_kernel(
-    packed_ref, slots_ref, gw_ref, out_ref, gw_out,
+    from_ref, bags_ref, slots_ref, gw_ref, out_ref, gw_out, rows_ref, packed_ref,
     pk_recv, sl_recv, gw_recv, s1, r1, s2, r2, own, s3, r3, s4, r4,
     gs1, gr1, gs2, gr2, gown, gs3, gr3, gs4, gr4, send_sem, recv_sem,
 ):
@@ -278,20 +254,36 @@
     slot_copy = remote(slots_ref.at[other], sl_recv, 16, partner)
     gw_copy = remote(gw_ref.at[:, other], gw_recv, 17, partner)
     slot_copy.start()
-    order = [(2, dy) for dy in (0, 1, 2, 3)] + [(dx, 2) for dx in (0, 1, 3)]
-    order += [(dx, dy) for dx in (1, 3, 0) for dy in (1, 3, 0)]
+    gw_copy.start()
     pair = {}
-    for number, (dx, dy) in enumerate(order):
-        o = owner(0, dx, dy)
-        pair[dx, dy] = remote(packed_ref.at[other, o], pk_recv.at[o], number, partner)
-        pair[dx, dy].start()
-    gw_copy.start()
-    slot_copy.wait_recv()
     arrived = set()
+    part = 64
+
+    def gather(side, o):
+        row = (side * (OWNERS // 2) + o) * E
+
+        @pl.loop(0, CAP // part)
+        def _(t):
+            at = row + (t // 2) * (OWNERS * E) + lax.rem(t, 2) * part
+            for k in range(part):
+                rows_ref[pl.ds(t * part + k, 1), :] = bags_ref[pl.ds(from_ref[at + k], 1), :]
+
+        packed_ref[side, o] = rows_ref[...].astype(bf16)
+
+    def prepare(keys):
+        keys = [key for key in keys if key not in pair]
+        for key in keys:
+            o = owner(0, *key)
+            gather(other, o)
+            pair[key] = remote(packed_ref.at[other, o], pk_recv.at[o], len(pair), partner)
+            pair[key].start()
+        for key in keys:
+            gather(core, owner(0, *key))
 
     def need(phase, major, minors):
-        for minor in minors:
-            key = (major, minor) if phase == 0 else (minor, major)
+        keys = [(major, minor) if phase == 0 else (minor, major) for minor in minors]
+        prepare(keys)
+        for key in keys:
             if key not in arrived:
                 arrived.add(key)
                 pair[key].wait_recv()
@@ -328,14 +320,6 @@
         copies.append(c)
         return c
 
-    for phase in range(2):
-        need(phase, 2, range(4))
-        for j in range(4):
-            s1[phase, j] = block(phase, 2, j).astype(bf16)
-            c = copy1(phase, j)
-            c.start()
-            copies.append(c)
-
     gw_copy.wait_recv()
     g1 = {}
     for phase in range(2):
@@ -348,6 +332,17 @@
                 along_major(phase, 1 + 2 * way),
             )
             g1[phase, way].start()
+
+    slot_copy.wait_recv()
+    first = []
+    for phase in range(2):
+        need(phase, 2, range(4))
+        for j in range(4):
+            s1[phase, j] = block(phase, 2, j).astype(bf16)
+            c = copy1(phase, j)
+            c.start()
+            first.append(c)
+            copies.append(c)
 
     sent2 = {}
 
@@ -360,13 +355,17 @@
         sent2[phase, way, j] = copy2(phase, way, j)
         sent2[phase, way, j].start()
 
-    copies_by = {(phase, j): copies[phase * 4 + j] for phase in range(2) for j in range(4)}
-    for phase in range(2):
-        for way, j in ((0, 2), (1, 1), (0, 3), (1, 0)):
+    copies_by = {(phase, j): first[phase * 4 + j] for phase in range(2) for j in range(4)}
+    for phase in range(2):
+        order = ((0, 2), (1, 1), (0, 3), (1, 0))
+        prepare([(1 + 2 * way, j) if phase == 0 else (j, 1 + 2 * way) for way, j in order])
+        for way, j in order:
             need(phase, 1 + 2 * way, (j,))
             second(phase, way, j, False)
     for phase in range(2):
-        for way, j in ((1, 2), (0, 1), (1, 3), (0, 0)):
+        order = ((1, 2), (0, 1), (1, 3), (0, 0))
+        prepare([(1 + 2 * way, j) if phase == 0 else (j, 1 + 2 * way) for way, j in order])
+        for way, j in order:
             need(phase, 1 + 2 * way, (j,))
             second(phase, way, j, True)
     g2 = {}
@@ -458,7 +457,7 @@
         c.wait_send()
 
 
-def reduce_rows(packed, slots, grad_weight):
+def reduce_rows(source, bags, slots, grad_weight):
     vmem = pl.BlockSpec(memory_space=pltpu.VMEM)
     cols = grad_weight.shape[-1]
     halves = (HALF, E)
@@ -469,9 +468,11 @@
             jax.ShapeDtypeStruct((2 * HALF, E), f32),
             jax.ShapeDtypeStruct((2 * GW_HALF, cols), f32),
         ),
-        in_specs=[vmem, vmem, vmem],
+        in_specs=[pl.BlockSpec(memory_space=pltpu.SMEM), vmem, vmem, vmem],
         out_specs=(vmem, vmem),
         scratch_shapes=[
+            pltpu.VMEM((CAP, E), f32),
+            pltpu.VMEM((2, 16, CAP, E), bf16),
             pltpu.VMEM((16, CAP, E), bf16),
             pltpu.VMEM((16, 1, CAP), jnp.int32),
             pltpu.VMEM((16, 2 * GW_HALF, cols), f32),
@@ -498,21 +499,21 @@
         ],
         compiler_params=pltpu.CompilerParams(collective_id=0, has_side_effects=True),
         name="reduce_rows",
-    )(packed, slots, grad_weight)
+    )(source, bags, slots, grad_weight)
 
 
 def shards(grad_out, pooled, compress_w, owner_ids, slot_ids, touched, table, accum):
     chips = OWNERS // 2
-    bags, grad_weight, dest, slots = front(
+    bags, grad_weight, source, slots = front(
         grad_out,
         pooled[0, 0],
         compress_w[0],
         owner_ids.reshape(-1, E),
         slot_ids.reshape(-1, E),
     )
-    packed = pack(dest.reshape(-1), bags, OWNERS * CAP)
     row_grad, grad_weight = reduce_rows(
-        packed.reshape(2, chips, CAP, E),
+        source.reshape(-1),
+        bags,
         slots.reshape(2, chips, 1, CAP),
         grad_weight.reshape(chips, 2, -1, grad_weight.shape[1]),
     )

time: 78.6 us -> 78.5 us (level)
  local copies, waits for them, and re-layouts: 1.54 us -> 0 us
  Pallas kernels: 76.2 us -> 77.7 us
    pallas_call x1, Pallas kernels: 43.1 us -> 55.7 us  [reduce_rows(): pl.pallas_call(reduce_kernel, out_shape=(jax.ShapeDtypeStruct((2 * HALF,...]
    pallas_call x2 -> x1, Pallas kernels: 27.4 us -> 16.3 us  [front(): pl.pallas_call(front_kernel, out_shape=(jax.ShapeDtypeStruct((FEATS * gro...]
    reshape x1 -> x0, local copies, waits for them, and re-layouts: 1.54 us -> none  [shards(): slots.reshape(2, chips, 1, CAP)]
where the time goes in v4:
time: 78.5 us; the launch traced here: 78.3 us
  Pallas kernels  77.7 us (99%)
    pallas_call x1, Pallas kernels, reduce_rows(): pl.pallas_call(reduce_kernel, out_shape=(jax.ShapeDtypeStruct((2 * HALF,...  55.7 us
    pallas_call x1, Pallas kernels, front(): pl.pallas_call(front_kernel, out_shape=(jax.ShapeDtypeStruct((FEATS * gro...  16.3 us
    pallas_call x1, Pallas kernels, update(): pl.pallas_call(update_kernel, out_shape=(jax.ShapeDtypeStruct(table.shape...  5.64 us

profile of v4, /device:TPU:1, one launch (start us, length us, event | category | flops | bytes accessed | tf_op | source)
XLA Modules:
  0.0 78.3 jit_solution(5959468246219095243)
XLA Ops:
  0.6 16.3 %front.1 = (f32[2056,128]{1,0:T(8,128)}, f32[1024,256]{1,0:T(8,128)}, s32[128,128]{1,0:T(8,128)}, s32[32,1,512]{2,1,0:T(1,128)}) custom-call(bf16[32,8,256]{2,1,0:T(8,128)(2,1)} %grad_ref.1, bf16[256,1024]{1,0:T(8,128)(2,1)} %bitcast.16, bf16[1024,256]{1,0:T(8,128)(2,1)} %bitcast.17, s32[64,128]{1,0:T(8,128)} %bitcast.20, s32[64,128]{1,0:T(8,128)} %bitcast.21), custom_call_target="tpu_custom_call" | custom-call | tf_op jit(solution)/shard_map/front/pallas_call | solution.py:138
  17.0 55.7 %reduce_rows.1 = (f32[1024,128]{1,0:T(8,128)}, f32[32,256]{1,0:T(8,128)}) custom-call(s32[16384]{0:T(1024)} %bitcast.18, f32[2056,128]{1,0:T(8,128)} %get-tuple-element.13.bags_ref, s32[2,16,1,512]{3,2,1,0:T(1,128)} %bitcast.19, f32[16,2,32,256]{3,2,1,0:T(8,128)} %bitcast.15), custom_call_target="tpu_custom_call" | custom-call | tf_op jit(solution)/shard_map/reduce_rows/pallas_call | solution.py:465
  72.7 5.6 %row_update.1 = (f32[4096,128]{1,0:T(8,128)}, f32[32,128]{1,0:T(8,128)}, f32[32,256]{1,0:T(8,128)}) custom-call(s32[1024]{0:T(1024)} %bitcast.23, s32[8,128]{1,0:T(8,128)} %bitcast.24, f32[1024,128]{1,0:T(8,128)} %get-tuple-element.16.grad_ref, f32[4096,128]{1,0:T(8,128)} %bitcast.14, f32[32,128]{1,0:T(8,128)} %bitcast.22, f32[32,256]{1,0:T(8,128)} %get-tuple-element.17.gw_ref), custom_call_target="tpu_custom_call" | custom-call | tf_op jit(solution)/shard_map/row_update/pallas_call | solution.py:198
